TPU v7x, 512 devices: a whole 4x4x16 slice. The times are simulated.
512 devices in a mesh: dp: 16 (over z), tensor: 32 (over x, y, core).
Axes of the slice: x: 4, y: 4, z: 16, core: 2. Of those that a mesh axis runs over, the one named last changes fastest.
Arguments:
- pages: bfloat16 [2, 64, 64, 2048], P(None, 'dp', None, 'tensor'), may hold values from -8 to 8
- page_table: int32 [16, 2], replicated, may hold values from 0 to 63, as said below
- page_count: int32 [16], replicated, may hold values from 1 to 2
- last_len: int32 [16], replicated, may hold values from 1 to 64
- targets: int32 [16, 128], P('dp'), may hold values from 0 to 65535
- mix_key: float32 [2, 2048], P(None, 'tensor'), may hold values from 0.05 to 0.95
- w_key: bfloat16 [2, 2048, 8192], P(None, None, 'tensor'), may hold values from -0.125 to 0.125
- w_value: bfloat16 [2, 8192, 2048], P(None, 'tensor'), may hold values from -0.0625 to 0.0625
- ln_gain: float32 [2, 2048], replicated, may hold values from 0.5 to 1.5
- ln_bias: float32 [2, 2048], replicated, may hold values from -2 to 2
- head: bfloat16 [2, 2048, 65536], P(None, 'dp', 'tensor'), may hold values from -8 to 8
Outputs:
- token_logprob: float32 [16, 128], P('dp', 'tensor')
- ratio_sum: float32 [16], P('dp')
Inputs may be any that keep to these rules, and one draw needn't show every extreme that they name: Entries are distinct; the page lives on dp device page_table[r, p] // 4.
All inputs are finite; a program needn't handle non-finite values.
Results may differ from a plain program's by a relative error of at most 0.0029.
The roundings to bfloat16 on the way count: a program that leaves them out, or rounds other values in their place, can miss the bound.
Values may be sent and summed in bfloat16 or wider, within the bound.
A program may use at most 128 MiB of HBM per device.

v0:
```python
import jax
import jax.numpy as jnp
from jax import lax
from jax.sharding import PartitionSpec as P

D = 2048


epsilon = 1e-05


def joined(value, axis, join):
    pieces = jax.tree.map(lambda part: lax.all_gather(part, axis), value)
    head = jax.tree.map(lambda part: part[0], pieces)
    tail = jax.tree.map(lambda part: part[1:], pieces)
    total, _ = lax.scan(lambda total, piece: (join(total, piece), None), head, tail)
    return total


def combine(left_stats, right_stats):
    peak = jnp.maximum(left_stats[0], right_stats[0])
    totals = left_stats[1] * jnp.exp(left_stats[0] - peak) + right_stats[1] * jnp.exp(
        right_stats[0] - peak
    )
    return (peak, totals, left_stats[2] + right_stats[2])


def body(
    pages,
    page_table,
    page_count,
    last_len,
    targets,
    mix_key,
    w_key,
    w_value,
    ln_gain,
    ln_bias,
    head,
):
    tensor_count = lax.axis_size("tensor")
    owner = lax.axis_index("dp")
    tensor_index = lax.axis_index("tensor")
    page_len = pages.shape[2]
    width_local = pages.shape[3]
    page_cap = page_table.shape[1]
    slot_count = page_cap * page_len
    live_pages = jnp.arange(page_cap)[None, :] < page_count[:, None]
    table_row = page_table[owner]
    everything = lax.all_gather(pages, "dp", axis=1, tiled=True)
    states = jnp.take(everything, table_row, axis=1)
    states = jnp.where(live_pages[owner][None, :, None, None], states, jnp.zeros_like(states))
    states = states.reshape(2, slot_count, width_local)
    state_f = states.astype(jnp.float32)
    previous = jnp.concatenate(
        [jnp.zeros((2, 1, width_local), jnp.float32), state_f[:, :-1]], axis=1
    )
    shifted = (state_f + (previous - state_f) * mix_key[:, None, :]).astype(jnp.bfloat16)
    hidden = jnp.einsum(
        "msd,mdf->msf",
        lax.all_gather(shifted, "tensor", axis=2, tiled=True),
        w_key,
        preferred_element_type=jnp.float32,
    )
    key_act = (jnp.maximum(hidden, 0.0) ** 2).astype(jnp.bfloat16)
    partial_out = jnp.einsum("msf,mfd->msd", key_act, w_value, preferred_element_type=jnp.float32)
    ffn_out = lax.psum_scatter(partial_out, "tensor", scatter_dimension=2, tiled=True)
    residual = state_f + ffn_out
    row_sum, row_square = lax.psum(
        (jnp.sum(residual, axis=-1), jnp.sum(residual * residual, axis=-1)), "tensor"
    )
    average = row_sum / D
    variance = row_square / D - average * average
    gain_local = lax.dynamic_slice_in_dim(ln_gain, tensor_index * width_local, width_local, 1)
    bias_local = lax.dynamic_slice_in_dim(ln_bias, tensor_index * width_local, width_local, 1)
    normed_local = (
        (residual - average[..., None])
        * lax.rsqrt(variance + epsilon)[..., None]
        * gain_local[:, None, :]
        + bias_local[:, None, :]
    ).astype(jnp.bfloat16)
    normed = lax.all_gather(normed_local, "tensor", axis=2, tiled=True)
    vocab_local = head.shape[2]
    logits = jnp.einsum(
        "msd,mdv->msv",
        normed,
        lax.all_gather(head, "dp", axis=1, tiled=True),
        preferred_element_type=jnp.float32,
    )
    peak = jnp.max(logits, axis=-1)
    totals = jnp.sum(jnp.exp(logits - peak[..., None]), axis=-1)
    vocab_ids = jnp.arange(vocab_local) + tensor_index * vocab_local
    matches = vocab_ids[None, None, :] == targets[0][None, :, None]
    target_logit = jnp.sum(jnp.where(matches, logits, 0.0), axis=-1)
    peak, totals, target_logit = joined((peak, totals, target_logit), "tensor", combine)
    logp = target_logit - peak - jnp.log(totals)
    length = (page_count[owner] - 1) * page_len + last_len[owner]
    valid = jnp.arange(slot_count) < length
    policy_row = jnp.where(valid, logp[0], 0.0)
    ratio = jnp.sum(jnp.where(valid, logp[0] - logp[1], 0.0))
    share = slot_count // tensor_count
    token_part = lax.dynamic_slice_in_dim(policy_row, tensor_index * share, share)[None, :]
    return (token_part, ratio[None])


def solution(mesh):
    placed = (
        P(None, "dp", None, "tensor"),
        P(),
        P(),
        P(),
        P("dp", None),
        P(None, "tensor"),
        P(None, None, "tensor"),
        P(None, "tensor", None),
        P(),
        P(),
        P(None, "dp", "tensor"),
    )
    return jax.shard_map(
        body, mesh=mesh, in_specs=placed, out_specs=(P("dp", "tensor"), P("dp")), check_vma=False
    )
```

profile of v0, /device:TPU:1, one launch (start us, length us, event | category | flops | bytes accessed | tf_op | source)
XLA Modules:
  0.0 654.3 jit_solution(647617080670465465)
XLA Ops:
  7.2 0.0 copy-start
  7.2 0.0 all-gather.11.cloned.1.call-start
  7.2 0.7 all-gather.11.cloned.1.call-update
  7.9 0.0 all-gather.13.cloned.1.call-start
  8.0 0.9 dynamic-slice_reduce_fusion
  8.8 1.2 dynamic_slice.31
  10.1 0.7 compare_bitcast_fusion
  10.7 0.1 broadcast_in_dim.65
  10.8 0.1 broadcast_in_dim.66
  10.9 0.1 broadcast_in_dim.68
  11.0 0.1 broadcast_in_dim.69
  11.1 68.5 %all-gather.11.cloned.1.call-done = bf16[2,64,64,64]{3,2,1,0:T(8,128)(2,1)} async-done(((bf16[2,4,64,64]{3,2,1,0:T(8,128)(2,1)}), bf16[2,64,64,64]{3,2,1,0:T(8,128)(2,1)}) %all-gather.11.cloned.1.call-update) | async-done | bytes 1048592 | tf_op jit(solution)/shard_map/all_gather | solution.py:50
  79.6 2.2 gather_fusion
  81.7 0.1 copy.15
  81.8 0.1 gather.7
  81.9 1.4 add_convert_fusion.1
  83.3 0.0 all-gather.13.cloned.1.call-update
  83.4 0.0 reduce-scatter.2.cloned.1.call-start
  83.4 64.8 %all-gather.13.cloned.1.call-done = bf16[2,128,2048]{1,2,0:T(8,128)(2,1)} async-done(((bf16[2,128,64]{1,2,0:T(8,128)(2,1)}), bf16[2,128,2048]{1,2,0:T(8,128)(2,1)}) %all-gather.13.cloned.1.call-update) | async-done | bytes 1048592 | tf_op jit(solution)/shard_map/all_gather | solution.py:61
  148.2 0.0 copy-done
  148.2 4.5 fusion.4
  152.7 0.0 copy-start.2
  152.7 0.0 copy-start.1
  152.7 0.0 reduce-scatter.2.cloned.1.call-update
  152.7 0.0 all-gather.15.cloned.1.call-start
  152.8 0.8 constant_dynamic-slice_fusion.1
  153.6 98.6 %reduce-scatter.2.cloned.1.call-done = f32[2,128,64]{1,2,0:T(8,128)} async-done(((f32[2,128,2048]{1,2,0:T(8,128)}), f32[2,128,64]{1,2,0:T(8,128)}) %reduce-scatter.2.cloned.1.call-update) | async-done | bytes 65552 | tf_op jit(solution)/shard_map/reduce_scatter | solution.py:67
  252.1 0.9 fusion.6
  253.0 64.3 %all-reduce.1 = (f32[2,128]{1,0:T(2,128)S(1)}, f32[2,128]{1,0:T(2,128)S(1)}) all-reduce(f32[2,128]{1,0:T(2,128)S(1)} %get-tuple-element.47, f32[2,128]{1,0:T(2,128)S(1)} %get-tuple-element.46), channel_id=1, replica_groups=mesh['dp'=16,'tensor'=32] {'tensor'}, use_global_device_ids=true, to_apply=%region_4.5 | all-reduce | flops 512 | bytes 4096 | tf_op jit(solution)/shard_map/psum | solution.py:69
  317.3 1.6 add_convert_fusion
  318.9 0.0 all-gather.15.cloned.1.call-update
  318.9 0.0 all-gather.17.cloned.1.call-start
  319.0 0.5 all-gather.17.cloned.1.call-update
  320.2 0.0 copy-done.2
  320.2 0.6 dynamic_slice.32
  321.4 0.0 copy-done.1
  321.4 0.2 broadcast_compare_fusion
  321.7 53.0 %all-gather.15.cloned.1.call-done = bf16[2,128,2048]{1,2,0:T(8,128)(2,1)} async-done(((bf16[2,128,64]{1,2,0:T(8,128)(2,1)}), bf16[2,128,2048]{1,2,0:T(8,128)(2,1)}) %all-gather.15.cloned.1.call-update) | async-done | bytes 1048592 | tf_op jit(solution)/shard_map/all_gather | solution.py:82
  374.6 191.1 %all-gather.17.cloned.1.call-done = bf16[2,2048,2048]{2,1,0:T(8,128)(2,1)} async-done(((bf16[2,128,2048]{2,1,0:T(8,128)(2,1)}), bf16[2,2048,2048]{2,1,0:T(8,128)(2,1)}) %all-gather.17.cloned.1.call-update) | async-done | bytes 16777232 | tf_op jit(solution)/shard_map/all_gather | solution.py:87
  565.7 8.6 %fusion.11 = (f32[2,128]{1,0:T(2,128)S(1)}, f32[2,128,2048]{2,1,0:T(8,128)S(1)}) fusion(bf16[2,128,2048]{1,2,0:T(8,128)(2,1)} %all-gather.15.cloned.1.call-done, bf16[2,2048,2048]{2,1,0:T(8,128)(2,1)} %all-gather.17.cloned.1.call-done), kind=kOutput, calls=%fused_computation.45 | convolution fusion | flops 2148007680 | bytes 19923968 | tf_op jit(solution)/shard_map/msd,mdv->msv/dot_general | solution.py:84
  574.4 0.7 select_reduce_fusion
  575.1 24.7 %all-gather.5 = f32[32,2,128]{2,1,0:T(2,128)S(1)} all-gather(f32[1,2,128]{2,1,0:T(2,128)S(1)} %bitcast.56), channel_id=4, replica_groups=mesh['dp'=16,'tensor'=32] {'tensor'}, dimensions={0}, use_global_device_ids=true | all-gather | bytes 33792 | tf_op jit(solution)/shard_map/all_gather | solution.py:13
  599.8 23.5 %all-gather.4 = f32[32,2,128]{2,1,0:T(2,128)S(1)} all-gather(f32[1,2,128]{2,1,0:T(2,128)S(1)} %bitcast.55), channel_id=3, replica_groups=mesh['dp'=16,'tensor'=32] {'tensor'}, dimensions={0}, use_global_device_ids=true | all-gather | bytes 33792 | tf_op jit(solution)/shard_map/all_gather | solution.py:13
  623.3 21.9 %all-gather.3 = f32[32,2,128]{2,1,0:T(2,128)S(1)} all-gather(f32[1,2,128]{2,1,0:T(2,128)S(1)} %bitcast.54), channel_id=2, replica_groups=mesh['dp'=16,'tensor'=32] {'tensor'}, dimensions={0}, use_global_device_ids=true | all-gather | bytes 33792 | tf_op jit(solution)/shard_map/all_gather | solution.py:13
  645.2 1.3 while.14
  646.5 0.6 fusion.7
  647.1 0.6 dynamic-slice_bitcast_fusion
  (44 shorter events, 1.0 us)
Async XLA Ops:
  7.2 141.0 %copy-start = (bf16[2,256,2048]{2,1,0:T(8,128)(2,1)S(1)}, bf16[2,256,2048]{2,1,0:T(8,128)(2,1)}, u32[]{:S(2)}) copy-start(bf16[2,256,2048]{2,1,0:T(8,128)(2,1)} %param.20) | copy-start | bytes 6291460
  7.2 72.4 %all-gather.11.cloned.1.call-start = ((), (), s32[]{:S(2)}) async-start(), calls=%async_computation.1 | async-start | bytes 2228224 | tf_op jit(solution)/shard_map/all_gather | solution.py:50
  7.9 140.3 %all-gather.13.cloned.1.call-start = ((), (), s32[]{:S(2)}) async-start(), calls=%async_computation.2 | async-start | bytes 1081344 | tf_op jit(solution)/shard_map/all_gather | solution.py:61
  83.4 168.8 %reduce-scatter.2.cloned.1.call-start = ((), (), s32[]{:S(2)}) async-start(), calls=%async_computation.3 | async-start | bytes 2162688 | tf_op jit(solution)/shard_map/reduce_scatter | solution.py:67
  152.7 167.5 %copy-start.2 = (s32[16]{0:T(128)S(1)}, s32[16]{0:T(128)}, u32[]{:S(2)}) copy-start(s32[16]{0:T(128)} %param.16) | copy-start | bytes 196
  152.7 168.7 %copy-start.1 = (s32[1,128]{1,0:T(1,128)S(1)}, s32[1,128]{1,0:T(1,128)}, u32[]{:S(2)}) copy-start(s32[1,128]{1,0:T(1,128)} %param.17) | copy-start | bytes 1540
  152.7 221.9 %all-gather.15.cloned.1.call-start = ((), (), s32[]{:S(2)}) async-start(), calls=%async_computation.4 | async-start | bytes 1081344 | tf_op jit(solution)/shard_map/all_gather | solution.py:82
  318.9 246.8 %all-gather.17.cloned.1.call-start = ((), (), s32[]{:S(2)}) async-start(), calls=%async_computation.5 | async-start | bytes 17825792 | tf_op jit(solution)/shard_map/all_gather | solution.py:87
Sparse Core Ops, SparseCore 0:
  10.1 69.4 all-gather.10
  83.5 64.6 all-gather.12
  152.9 99.2 reduce-scatter.1
  319.0 55.5 all-gather.14
  376.5 189.1 all-gather.16
where the time goes:
time: 655 us; the launch traced here: 654 us
  waiting for transfers between devices  477 us (73%)
  blocking collectives  134 us (20%)
  between operations  15.2 us (2%)
  matrix products  13.2 us (2%)
  other arithmetic  6.97 us (1%)
  local copies, waits for them, and re-layouts  6.76 us (1%)
    all_gather x1, waiting for transfers between devices, body(): lax.all_gather(head, 'dp', axis=1, tiled=True)  191 us
    reduce_scatter x1, waiting for transfers between devices, body(): lax.psum_scatter(partial_out, 'tensor', scatter_dimension=2, tiled=True)  98.6 us
    all_gather x3, blocking collectives, joined(): pieces = jax.tree.map(lambda part: lax.all_gather(part, axis), value)  70.1 us
    all_gather x1, waiting for transfers between devices, body(): everything = lax.all_gather(pages, 'dp', axis=1, tiled=True)  68.5 us
    all_gather x1, waiting for transfers between devices, body(): lax.all_gather(shifted, 'tensor', axis=2, tiled=True)  64.8 us
    psum x1, blocking collectives, body(): lax.psum((jnp.sum(residual, axis=-1), jnp.sum(residual * residual, axis=-...  64.3 us
    all_gather x1, waiting for transfers between devices, body(): normed = lax.all_gather(normed_local, 'tensor', axis=2, tiled=True)  53 us
  transfers between devices with their start and end apart: 5, of which 5 were waited for; matrix products, arithmetic and copies ran while one was open for 1% of the time, Pallas kernels for 0%

commit v1 on v0

v1 whole, which is shorter than its diff:
```python
import functools

import jax
import jax.numpy as jnp
from jax import lax
from jax.experimental import pallas as pl
from jax.experimental.pallas import tpu as pltpu
from jax.sharding import PartitionSpec as P

epsilon = 1e-05
F32 = jnp.float32
BF16 = jnp.bfloat16
LANES = 128


def iota(shape, axis):
    return lax.broadcasted_iota(jnp.int32, shape, axis)


def rows_of(*rows):
    place = iota((8, LANES), 0)
    tile = jnp.zeros((8, LANES), F32)
    for index, row in enumerate(rows):
        tile = jnp.where(place == index, jnp.broadcast_to(row, (8, LANES)), tile)
    return tile


def column_of(row):
    return jnp.broadcast_to(row, (LANES, LANES)).T


def kernel(
    nz,
    side,
    table_ref,
    count_ref,
    last_ref,
    pages_ref,
    mix_ref,
    target_ref,
    gain_ref,
    bias_ref,
    wk_hbm,
    wv_hbm,
    head_hbm,
    out_ref,
    pages_in,
    mix_in,
    targets_all,
    head_src,
    head_own,
    head_all,
    wk_all,
    wv_all,
    window,
    chosen,
    picked,
    shifted_all,
    act,
    partial,
    summed,
    stats,
    sets,
    tokens,
    logits,
    local_stats,
    column_stats,
    plane_stats,
    logp_pair,
    pair_send,
    pair_recv,
    load_sem,
    tgt_send,
    tgt_recv,
    win_send,
    win_recv,
    pick_send,
    pick_recv,
    shift_send,
    shift_recv,
    sum_send,
    sum_recv,
    stat_send,
    stat_recv,
    hz_send,
    hz_recv,
    hx_send,
    hx_recv,
    set_send,
    set_recv,
    near_send,
    near_recv,
    tok_send,
    tok_recv,
    c0_send,
    c0_recv,
    c1_send,
    c1_recv,
):
    chips = side * side
    per_set = nz // side
    z = lax.axis_index("dp")
    tensor = lax.axis_index("tensor")
    core = lax.rem(tensor, 2)
    chip = tensor // 2
    x = chip // side
    y = lax.rem(chip, side)
    my_set = lax.rem(x + y, side)
    z_set = lax.rem(z, side)
    sign = 1 - 2 * core
    width = chips * LANES
    units = wk_hbm.shape[2]
    vocab_half = head_hbm.shape[2]
    rows = head_hbm.shape[1]
    slots = nz // 2
    near = {4: (1, -1, 2), 2: (1,)}[side]

    def remote(src, dst, send, recv, to_z, to_chip, to_core):
        return pltpu.make_async_remote_copy(
            src_ref=src,
            dst_ref=dst,
            send_sem=send,
            recv_sem=recv,
            device_id={"dp": to_z, "tensor": to_chip * 2 + to_core},
            device_id_type=pl.DeviceIdType.MESH,
        )

    def wrap(value, size):
        return lax.rem(value + 4 * size, size)

    def lane(index):
        return pl.ds(pl.multiple_of(index * LANES, LANES), LANES)

    unit_cols = pl.ds(pl.multiple_of(core * units, units), units)
    loads = (
        pltpu.make_async_copy(wk_hbm.at[core], wk_all.at[:, unit_cols], load_sem.at[0]),
        pltpu.make_async_copy(wv_hbm.at[core], wv_all.at[unit_cols, :], load_sem.at[1]),
        pltpu.make_async_copy(head_hbm.at[core], head_src.at[core], load_sem.at[2]),
    )
    for load in loads:
        load.start()

    barrier = pltpu.get_barrier_semaphore()

    def hello(to_z, to_chip, to_core):
        pl.semaphore_signal(
            barrier,
            inc=1,
            device_id={"dp": to_z, "tensor": to_chip * 2 + to_core},
            device_id_type=pl.DeviceIdType.MESH,
        )

    hello(z, chip, 1 - core)

    def hello_z(step, carry):
        hello(wrap(z + step, nz), chip, core)
        return carry

    def hello_plane(step, carry):
        hello(z, wrap(chip + step, chips), core)
        return carry

    lax.fori_loop(1, nz, hello_z, 0)
    lax.fori_loop(1, chips, hello_plane, 0)
    pl.semaphore_wait(barrier, nz - 1 + chips - 1 + 1)

    other = 1 - core
    pair = (
        remote(pages_ref.at[other], pages_in, pair_send.at[0], pair_recv.at[0], z, chip, other),
        remote(mix_ref.at[other], mix_in, pair_send.at[1], pair_recv.at[1], z, chip, other),
        remote(
            head_hbm.at[other], head_src.at[core], pair_send.at[2], pair_recv.at[2], z, chip, other
        ),
        remote(
            wk_hbm.at[other],
            wk_all.at[:, unit_cols],
            pair_send.at[3],
            pair_recv.at[3],
            z,
            chip,
            other,
        ),
        remote(
            wv_hbm.at[other],
            wv_all.at[unit_cols, :],
            pair_send.at[4],
            pair_recv.at[4],
            z,
            chip,
            other,
        ),
    )
    for copy in pair:
        copy.start()

    pair[0].wait_recv()
    window[pl.ds(4, 4)] = pages_ref[core] + pages_in[...]
    window_offsets = {4: (-1, 0, 1, 2), 2: (-1, 0)}[side]
    mine = window.at[pl.ds(4, 4)]
    moves = []
    for slot, offset in enumerate(window_offsets):
        if offset == 0:
            continue
        copy = remote(
            mine,
            window.at[pl.ds(slot * 4, 4)],
            win_send.at[slot],
            win_recv.at[slot],
            wrap(z - sign * offset, nz),
            chip,
            core,
        )
        copy.start()
        moves.append(copy)
    targets_all[z] = target_ref[...]

    def send_target(step, carry):
        remote(
            target_ref,
            targets_all.at[z],
            tgt_send.at[step],
            tgt_recv.at[step],
            wrap(z + step, nz),
            chip,
            core,
        ).start()
        return carry

    lax.fori_loop(1, nz, send_target, 0)
    for copy in moves:
        copy.wait_recv()

    picks = []
    for step in range(per_set):
        to_z = wrap(z + side * step, nz)
        for page in range(2):
            entry = table_ref[to_z, page]
            slot = lax.rem((entry // 4 - z) * sign + 1 + 4 * nz, nz)
            wanted = jnp.logical_and(slot < side, page < count_ref[to_z])
            flag = jnp.where(wanted, 1.0, 0.0).astype(F32)
            index = jnp.minimum(slot, side - 1) * 4 + lax.rem(entry, 4)
            block = (window[index].astype(F32) * flag).astype(BF16)
            if step == 0:
                picked[0, page] = block
            else:
                chosen[step, page] = block
        if step > 0:
            copy = remote(
                chosen.at[step],
                picked.at[step],
                pick_send.at[step],
                pick_recv.at[step],
                to_z,
                chip,
                core,
            )
            copy.start()
            picks.append(copy)

    loads[2].wait()
    pair[2].wait_recv()

    def head_piece(to_z):
        start = pl.multiple_of(lax.rem(to_z, slots) * 2 * LANES, 2 * LANES)
        return head_src.at[to_z // slots, :, pl.ds(start, 2 * LANES)]

    def head_rows(index):
        return pl.ds(pl.multiple_of(index * rows, rows), rows)

    def head_copy(step):
        to_z = wrap(z + step, nz)
        return remote(
            head_piece(to_z),
            head_own.at[head_rows(z), :],
            hz_send.at[step],
            hz_recv.at[step],
            to_z,
            chip,
            core,
        )

    def head_start(step, carry):
        head_copy(step).start()
        return carry

    lax.fori_loop(1, nz, head_start, 0)
    keep = pltpu.make_async_copy(head_piece(z), head_own.at[head_rows(z), :], load_sem.at[3])
    keep.start()

    pair[1].wait_recv()
    for copy in picks:
        copy.wait_recv()
    state = picked[0].astype(F32)
    for step in range(1, per_set):
        state = state + picked[step].astype(F32)
    state = state.reshape(LANES, LANES)
    rolled = pltpu.roll(state, 1, 0)
    previous = jnp.where(iota((LANES, LANES), 0) == 0, 0.0, rolled)
    mix = mix_ref[core, 0:1, :] + mix_in[0:1, :]
    shifted_all[:, lane(chip)] = (state + (previous - state) * mix).astype(BF16)

    def shift_copy(step, source, to_chip):
        return remote(
            shifted_all.at[:, lane(source)],
            shifted_all.at[:, lane(source)],
            shift_send.at[step],
            shift_recv.at[step],
            z,
            to_chip,
            core,
        )

    def shift_start(step, carry):
        shift_copy(step, chip, wrap(chip + step, chips)).start()
        return carry

    lax.fori_loop(1, chips, shift_start, 0)

    def shift_wait(step, carry):
        shift_copy(step, wrap(chip - step, chips), chip).wait_recv()
        return carry

    loads[0].wait()
    loads[1].wait()
    pair[3].wait_recv()
    pair[4].wait_recv()
    lax.fori_loop(1, chips, shift_wait, 0)

    hidden = jnp.dot(shifted_all[...], wk_all[...], preferred_element_type=F32)
    act[...] = (jnp.maximum(hidden, 0.0) ** 2).astype(BF16)

    def sum_copy(source, to_chip):
        return remote(
            partial.at[to_chip],
            summed.at[source],
            sum_send.at[to_chip],
            sum_recv.at[source],
            z,
            to_chip,
            core,
        )

    def mix_out(step, carry):
        block = lax.rem(chip // 2 + 1 + step, chips // 2)
        cols = pl.ds(pl.multiple_of(block * 2 * LANES, 2 * LANES), 2 * LANES)
        part = jnp.dot(act[...], wv_all[:, cols], preferred_element_type=F32)
        partial[block * 2] = part[:, :LANES]
        partial[block * 2 + 1] = part[:, LANES:]
        for lower in range(2):
            to_chip = block * 2 + lower

            @pl.when(to_chip != chip)
            def _():
                sum_copy(chip, to_chip).start()

        return carry

    lax.fori_loop(0, chips // 2, mix_out, 0)

    def sum_in(step, total):
        source = wrap(chip + step, chips)
        sum_copy(source, chip).wait_recv()
        return total + summed[source]

    residual = lax.fori_loop(1, chips, sum_in, state + partial[chip])

    turned = residual.T
    stats[chip] = rows_of(
        jnp.sum(turned, axis=0, keepdims=True), jnp.sum(turned * turned, axis=0, keepdims=True)
    )

    def stat_copy(step, source, to_chip):
        return remote(
            stats.at[source],
            stats.at[source],
            stat_send.at[step],
            stat_recv.at[step],
            z,
            to_chip,
            core,
        )

    def stat_start(step, carry):
        stat_copy(step, chip, wrap(chip + step, chips)).start()
        return carry

    def stat_wait(step, carry):
        stat_copy(step, wrap(chip - step, chips), chip).wait_recv()
        return carry

    lax.fori_loop(1, chips, stat_start, 0)
    lax.fori_loop(1, chips, stat_wait, 0)
    total = jnp.sum(stats[...], axis=0)
    average = total[0:1] / width
    variance = total[1:2] / width - average * average
    scale = lax.rsqrt(variance + epsilon)
    model = core.astype(F32)
    gains = gain_ref[:, lane(chip)]
    biases = bias_ref[:, lane(chip)]
    gain = gains[0:1] * (1.0 - model) + gains[1:2] * model
    bias = biases[0:1] * (1.0 - model) + biases[1:2] * model
    normed = (residual - column_of(average)) * column_of(scale) * gain + bias
    place = z // side
    sets[0, place] = normed.astype(BF16)

    sends = []
    for step in range(1, per_set):
        copy = remote(
            sets.at[0, place],
            sets.at[0, place],
            set_send.at[step],
            set_recv.at[step],
            wrap(z + side * step, nz),
            chip,
            core,
        )
        copy.start()
        sends.append(copy)

    def head_wait(step, carry):
        head_copy(step).wait_recv()
        return carry

    keep.wait()
    lax.fori_loop(1, nz, head_wait, 0)
    stays = (
        pltpu.make_async_copy(
            head_own.at[:, 0:LANES], head_all.at[:, lane(x)], load_sem.at[4]
        ),
        pltpu.make_async_copy(
            head_own.at[:, LANES : 2 * LANES], head_all.at[:, lane(side + y)], load_sem.at[5]
        ),
    )
    for stay in stays:
        stay.start()
    spread = []
    for step in range(1, side):
        spread.append(
            remote(
                head_own.at[:, 0:LANES],
                head_all.at[:, lane(x)],
                hx_send.at[0, step],
                hx_recv.at[0, step],
                z,
                wrap(x + step, side) * side + y,
                core,
            )
        )
        spread.append(
            remote(
                head_own.at[:, LANES : 2 * LANES],
                head_all.at[:, lane(side + y)],
                hx_send.at[1, step],
                hx_recv.at[1, step],
                z,
                x * side + wrap(y + step, side),
                core,
            )
        )
    for copy in spread:
        copy.start()

    for copy in sends:
        copy.wait_recv()
    nears = []
    for slot, offset in enumerate(near):
        copy = remote(
            sets.at[0],
            sets.at[slot + 1],
            near_send.at[slot],
            near_recv.at[slot],
            wrap(z - sign * offset, nz),
            chip,
            core,
        )
        copy.start()
        nears.append(copy)

    def token_copy(slot, source, to_chip):
        return remote(
            sets.at[slot],
            tokens.at[:, :, lane(source)],
            tok_send.at[to_chip],
            tok_recv.at[source],
            z,
            to_chip,
            core,
        )

    for slot in range(side):
        if slot > 0:
            nears[slot - 1].wait_recv()
        offset = 0 if slot == 0 else near[slot - 1]
        group = lax.rem(wrap(z + sign * offset, nz), side)
        for to_x in range(side):
            to_chip = to_x * side + wrap(group - to_x, side)

            @pl.when(to_chip == chip)
            def _():
                tokens[:, :, lane(chip)] = sets[slot]

            @pl.when(to_chip != chip)
            def _():
                token_copy(slot, chip, to_chip).start()

    def target_wait(step, carry):
        remote(
            target_ref,
            targets_all.at[wrap(z - step, nz)],
            tgt_send.at[step],
            tgt_recv.at[step],
            z,
            chip,
            core,
        ).wait_recv()
        return carry

    lax.fori_loop(1, nz, target_wait, 0)
    wanted = jnp.concatenate(
        [
            column_of(targets_all[my_set + side * step][0:1].astype(F32))
            for step in range(per_set)
        ],
        axis=0,
    )

    for stay in stays:
        stay.wait()
    for copy in spread:
        copy.wait_recv()

    def token_wait(step, carry):
        source = wrap(chip + step, chips)
        token_copy(0, source, chip).wait_recv()
        return carry

    lax.fori_loop(1, chips, token_wait, 0)

    count = per_set * LANES

    def make_logits(block, peak):
        cols = pl.ds(pl.multiple_of(block * 2 * LANES, 2 * LANES), 2 * LANES)
        part = jnp.dot(
            tokens[...].reshape(count, width), head_all[:, cols], preferred_element_type=F32
        )
        logits[block] = part
        return jnp.maximum(peak, jnp.maximum(part[:, :LANES], part[:, LANES:]))

    peak = lax.fori_loop(0, side, make_logits, jnp.full((count, LANES), -jnp.inf, F32))
    peak = jnp.max(peak, axis=1, keepdims=True)
    total = jnp.zeros((count, LANES), F32)
    hit = jnp.zeros((count, LANES), F32)
    column = iota((count, LANES), 1).astype(F32)
    for block in range(side):
        for half in range(2):
            part = logits[block, :, half * LANES : (half + 1) * LANES]
            total = total + jnp.exp(part - peak)
            index = block * 2 + half
            if index < side:
                base = (index * side + y) * 2 * vocab_half + z * 2 * LANES
            else:
                base = (x * side + index - side) * 2 * vocab_half + z * 2 * LANES + LANES
            hit = hit + jnp.where(wanted - base.astype(F32) == column, part, 0.0)
    total = jnp.sum(total, axis=1, keepdims=True)
    hit = jnp.sum(hit, axis=1, keepdims=True)
    column = iota((count, LANES), 1)
    packed = jnp.where(column == 0, peak, jnp.where(column == 1, total, hit))
    for step in range(per_set):
        turned = packed[step * LANES : (step + 1) * LANES].T
        local_stats[step] = turned[0:8]

    def column_copy(step, source, to_z):
        return remote(
            local_stats.at[step],
            column_stats.at[source],
            c0_send.at[step],
            c0_recv.at[source],
            to_z,
            chip,
            core,
        )

    for step in range(per_set):
        to_z = my_set + side * step

        @pl.when(to_z == z)
        def _():
            column_stats[z] = local_stats[step]

        @pl.when(to_z != z)
        def _():
            column_copy(step, z, to_z).start()

    def combine(parts):
        peaks = parts[:, 0:1, :]
        top = jnp.max(peaks, axis=0)
        sums = jnp.sum(parts[:, 1:2, :] * jnp.exp(peaks - top[None]), axis=0)
        return top, sums, jnp.sum(parts[:, 2:3, :], axis=0)

    def plane_copy(step, source_x, to_chip):
        return remote(
            plane_stats.at[source_x],
            plane_stats.at[source_x],
            c1_send.at[step],
            c1_recv.at[source_x],
            z,
            to_chip,
            core,
        )

    @pl.when(my_set == z_set)
    def _():
        def column_wait(step, carry):
            source = wrap(z + step, nz)
            column_copy(0, source, z).wait_recv()
            return carry

        lax.fori_loop(1, nz, column_wait, 0)
        plane_stats[x] = rows_of(*combine(column_stats[...]))

        def plane_start(step, carry):
            plane_copy(step, x, wrap(chip + step, chips)).start()
            return carry

        lax.fori_loop(1, chips, plane_start, 0)

    for source_x in range(side):
        source = source_x * side + wrap(z_set - source_x, side)

        @pl.when(source != chip)
        def _():
            plane_copy(0, source_x, chip).wait_recv()

    top, sums, hits = combine(plane_stats[...])
    logp = hits - top - jnp.log(sums)
    logp_pair[0] = jnp.broadcast_to(logp, (8, LANES))
    swap = remote(
        logp_pair.at[0], logp_pair.at[1], pair_send.at[5], pair_recv.at[5], z, chip, other
    )
    swap.start()
    swap.wait_recv()
    own = logp_pair[0, 0:1]
    theirs = logp_pair[1, 0:1]
    policy = own * (1.0 - model) + theirs * model
    base_logp = own * model + theirs * (1.0 - model)
    length = (count_ref[z] - 1) * 64 + last_ref[z]
    valid = iota((1, LANES), 1) < length
    row = jnp.where(valid, policy, 0.0)
    ratio = jnp.sum(jnp.where(valid, policy - base_logp, 0.0), axis=1, keepdims=True)
    out_ref[...] = rows_of(row, jnp.broadcast_to(ratio, (1, LANES)))

    for copy in pair + (swap,):
        copy.wait_send()
    for copy in moves + picks + sends + nears + spread:
        copy.wait_send()

    def drain_z(step, carry):
        head_copy(step).wait_send()
        remote(
            target_ref,
            targets_all.at[z],
            tgt_send.at[step],
            tgt_recv.at[step],
            z,
            chip,
            core,
        ).wait_send()
        return carry

    lax.fori_loop(1, nz, drain_z, 0)

    def drain_plane(step, carry):
        to_chip = wrap(chip + step, chips)
        shift_copy(step, chip, to_chip).wait_send()
        stat_copy(step, chip, to_chip).wait_send()
        sum_copy(chip, to_chip).wait_send()
        token_copy(0, chip, to_chip).wait_send()
        return carry

    lax.fori_loop(1, chips, drain_plane, 0)
    for step in range(per_set):

        @pl.when(my_set + side * step != z)
        def _():
            column_copy(step, z, z).wait_send()

    @pl.when(my_set == z_set)
    def _():
        def drain_stats(step, carry):
            plane_copy(step, x, wrap(chip + step, chips)).wait_send()
            return carry

        lax.fori_loop(1, chips, drain_stats, 0)


def body(
    nz,
    side,
    pages,
    page_table,
    page_count,
    last_len,
    targets,
    mix_key,
    w_key,
    w_value,
    ln_gain,
    ln_bias,
    head,
):
    chips = side * side
    per_set = nz // side
    width = chips * LANES
    units = w_key.shape[2]
    rows = head.shape[1]
    tensor = lax.axis_index("tensor")
    core = tensor % 2
    low = core == 0

    def placed(value):
        zero = jnp.zeros_like(value)
        return jnp.concatenate(
            [jnp.where(low, value, zero), jnp.where(low, zero, value)], axis=-1
        )

    pages_wide = placed(pages)
    mix_wide = jnp.broadcast_to(placed(mix_key)[:, None, :], (2, 8, LANES))
    target_rows = jnp.broadcast_to(targets, (8, LANES))
    smem = pl.BlockSpec(memory_space=pltpu.SMEM)
    vmem = pl.BlockSpec(memory_space=pltpu.VMEM)
    hbm = pl.BlockSpec(memory_space=pl.ANY)
    dma = pltpu.SemaphoreType.DMA
    semaphores = [6, 6, 6]
    semaphores += [nz] * 2 + [4] * 2 + [per_set] * 2
    semaphores += [chips] * 6
    semaphores += [nz] * 2 + [(2, side)] * 2
    semaphores += [per_set] * 2 + [side] * 2 + [chips] * 2
    semaphores += [per_set, nz] + [chips, side]
    result = pl.pallas_call(
        functools.partial(kernel, nz, side),
        out_shape=jax.ShapeDtypeStruct((8, LANES), F32),
        in_specs=[smem] * 3 + [vmem] * 5 + [hbm] * 3,
        out_specs=vmem,
        scratch_shapes=[
            pltpu.VMEM((4, 64, LANES), BF16),
            pltpu.VMEM((8, LANES), F32),
            pltpu.VMEM((nz, 8, LANES), jnp.int32),
            pltpu.VMEM((2, rows, head.shape[2]), BF16),
            pltpu.VMEM((width, 2 * LANES), BF16),
            pltpu.VMEM((width, 2 * side * LANES), BF16),
            pltpu.VMEM((width, 2 * units), BF16),
            pltpu.VMEM((2 * units, width), BF16),
            pltpu.VMEM((side * 4, 64, LANES), BF16),
            pltpu.VMEM((per_set, 2, 64, LANES), BF16),
            pltpu.VMEM((per_set, 2, 64, LANES), BF16),
            pltpu.VMEM((LANES, width), BF16),
            pltpu.VMEM((LANES, 2 * units), BF16),
            pltpu.VMEM((chips, LANES, LANES), F32),
            pltpu.VMEM((chips, LANES, LANES), F32),
            pltpu.VMEM((chips, 8, LANES), F32),
            pltpu.VMEM((side, per_set, LANES, LANES), BF16),
            pltpu.VMEM((per_set, LANES, width), BF16),
            pltpu.VMEM((side, per_set * LANES, 2 * LANES), F32),
            pltpu.VMEM((per_set, 8, LANES), F32),
            pltpu.VMEM((nz, 8, LANES), F32),
            pltpu.VMEM((side, 8, LANES), F32),
            pltpu.VMEM((2, 8, LANES), F32),
        ]
        + [dma(size if isinstance(size, tuple) else (size,)) for size in semaphores],
        compiler_params=pltpu.CompilerParams(
            collective_id=0, has_side_effects=True, vmem_limit_bytes=48 * 1024 * 1024
        ),
    )(
        page_table,
        page_count,
        last_len,
        pages_wide,
        mix_wide,
        target_rows,
        ln_gain,
        ln_bias,
        w_key,
        w_value,
        head,
    )
    share = LANES // (2 * chips)
    token_part = lax.dynamic_slice(result, (0, tensor * share), (1, share))
    return token_part, result[1, 0:1]


def solution(mesh):
    nz = mesh.shape["dp"]
    side = {32: 4, 8: 2}[mesh.shape["tensor"]]
    specs = (
        P(None, "dp", None, "tensor"),
        P(),
        P(),
        P(),
        P("dp", None),
        P(None, "tensor"),
        P(None, None, "tensor"),
        P(None, "tensor", None),
        P(),
        P(),
        P(None, "dp", "tensor"),
    )
    return jax.shard_map(
        functools.partial(body, nz, side),
        mesh=mesh,
        in_specs=specs,
        out_specs=(P("dp", "tensor"), P("dp")),
        check_vma=False,
    )
```

time: 655 us -> 173 us (0.26)
  waiting for transfers between devices: 477 us -> 0 us
  Pallas kernels: 0 us -> 160 us
  blocking collectives: 134 us -> 0 us
  between operations: 15.2 us -> 0.67 us
  matrix products: 13.2 us -> 0 us
    all_gather x4 -> x0, waiting for transfers between devices: 377 us -> none  [the longest x1 191 us: body(): lax.all_gather(head, 'dp', axis=1, tiled=True)]
    pallas_call x0 -> x1, Pallas kernels: none -> 160 us  [body(): pl.pallas_call(functools.partial(kernel, nz, side), out_shape=jax.ShapeDt...]
    reduce_scatter x1 -> x0, waiting for transfers between devices: 98.6 us -> none  [body(): lax.psum_scatter(partial_out, 'tensor', scatter_dimension=2, tiled=True)]
    all_gather x3 -> x0, blocking collectives: 70.1 us -> none  [joined(): pieces = jax.tree.map(lambda part: lax.all_gather(part, axis), value)]
    psum x1 -> x0, blocking collectives: 64.3 us -> none  [body(): lax.psum((jnp.sum(residual, axis=-1), jnp.sum(residual * residual, axis=-...]
    dot_general x2 -> x0, matrix products: 13.2 us -> none  [the longest x1 8.63 us: body(): jnp.einsum('msd,mdv->msv', normed, lax.all_gather(head, 'dp', axis=1, til...]
    unnamed x6 -> x15, local copies, waits for them, and re-layouts: 0.02 us -> 7.9 us
  transfers between devices with their start and end apart: 5 -> 0, of which waited for: 5 -> 0; matrix products, arithmetic and copies ran while one was open for 1% -> 0% of each run, Pallas kernels for 0% -> 0%
where the time goes in v1:
time: 173 us; the launch traced here: 172 us
  Pallas kernels  160 us (92%)
  local copies, waits for them, and re-layouts  9.66 us (6%)
  other arithmetic  1.8 us (1%)
    pallas_call x1, Pallas kernels, body(): pl.pallas_call(functools.partial(kernel, nz, side), out_shape=jax.ShapeDt...  160 us
    unnamed x15, local copies, waits for them, and re-layouts  7.9 us

profile of v1, /device:TPU:1, one launch (start us, length us, event | category | flops | bytes accessed | tf_op | source)
XLA Modules:
  0.0 172.5 jit_solution(16055644367084448305)
XLA Ops:
  0.6 0.9 broadcast_select_fusion.1
  1.6 0.1 pad_maximum_fusion.pages_ref
  1.7 0.7 broadcast_select_fusion.3
  2.4 0.1 pad_maximum_fusion.1
  2.5 0.8 copy.13.table_ref
  3.2 0.7 broadcast_in_dim.23.target_ref
  3.9 0.0 copy-start
  3.9 1.6 copy-done
  5.5 0.0 copy-start.1
  5.5 1.6 copy-done.1
  7.0 0.0 copy-start.2
  7.1 1.2 copy-done.2
  8.3 0.0 copy-start.3
  8.3 0.7 copy-done.3
  9.0 0.0 copy-start.4
  9.0 0.7 copy-done.4
  9.7 0.0 copy-start.5
  9.7 0.7 copy-done.5
  10.4 0.0 copy-start.6
  10.4 0.7 copy-done.6
  11.0 160.3 %shard_map.122 = f32[8,128]{1,0:T(8,128)S(1)} custom-call(s32[16,2]{1,0:T(8,128)S(1)} %copy.13.table_ref, s32[16]{0:T(128)S(1)} %copy-done.5, s32[16]{0:T(128)S(1)} %copy-done.6, bf16[2,4,64,128]{3,2,1,0:T(8,128)(2,1)S(1)} %pad_maximum_fusion.pages_ref, f32[2,8,128]{2,1,0:T(8,128)S(1)} %broadcast_in_dim.21.mix_ref, ...), custom_call_target="tpu_custom_call" | custom-call | tf_op jit(solution)/shard_map/pallas_call | solution.py:739
  171.4 0.6 constant_dynamic-slice_fusion
  171.9 0.5 slice.3
  (1 shorter events, 0.0 us)
Async XLA Ops:
  3.9 1.6 copy-start
  5.5 1.6 copy-start.1
  7.0 1.2 copy-start.2
  8.3 0.7 copy-start.3
  9.0 0.7 copy-start.4
  9.7 0.7 copy-start.5
  10.4 0.7 copy-start.6

commit v2 on v1

v2 whole, which is shorter than its diff:
```python
import functools

import jax
import jax.numpy as jnp
from jax import lax
from jax.experimental import pallas as pl
from jax.experimental.pallas import tpu as pltpu
from jax.sharding import PartitionSpec as P

epsilon = 1e-05
F32 = jnp.float32
BF16 = jnp.bfloat16
LANES = 128
BATCHES = {16: ((0, 8, 4, 12), (1, 15, 7, 9), (2, 14, 6, 10), (3, 13, 5, 11)), 4: ((0, 2), (1, 3))}
VMEM_LIMIT = 63 * 1024 * 1024


def iota(shape, axis):
    return lax.broadcasted_iota(jnp.int32, shape, axis)


def rows_of(*rows):
    place = iota((8, LANES), 0)
    tile = jnp.zeros((8, LANES), F32)
    for index, row in enumerate(rows):
        tile = jnp.where(place == index, jnp.broadcast_to(row, (8, LANES)), tile)
    return tile


def column_of(row):
    return jnp.broadcast_to(row, (LANES, LANES)).T


def kernel(
    nz,
    side,
    table_hbm,
    count_hbm,
    last_hbm,
    pages_hbm,
    mix_hbm,
    target_hbm,
    gain_hbm,
    bias_hbm,
    wk_hbm,
    wv_hbm,
    head_hbm,
    token_out,
    ratio_out,
    table_ref,
    count_ref,
    last_ref,
    pages_ref,
    mix_ref,
    gain_ref,
    bias_ref,
    pages_in,
    mix_in,
    targets_all,
    head_src,
    head_all,
    wk_all,
    wv_all,
    window,
    chosen,
    picked,
    shift_blocks,
    shifted_all,
    act,
    partial,
    line_sums,
    line_total,
    cross_sums,
    stats,
    sets,
    tokens,
    logits,
    local_stats,
    column_stats,
    plane_stats,
    pair_send,
    pair_recv,
    load_sem,
    tgt_send,
    tgt_recv,
    win_send,
    win_recv,
    pick_send,
    pick_recv,
    sa_send,
    sa_recv,
    sb_send,
    sb_recv,
    ra_send,
    ra_recv,
    rb_send,
    rb_recv,
    stat_send,
    stat_recv,
    hz_send,
    hz_recv,
    hf_send,
    hf_recv,
    hr_send,
    hr_recv,
    set_send,
    set_recv,
    near_send,
    near_recv,
    ta_send,
    ta_recv,
    tb_send,
    tb_recv,
    tr_send,
    tr_recv,
    c0_send,
    c0_recv,
    c1_send,
    c1_recv,
):
    chips = side * side
    per_set = nz // side
    z = lax.axis_index("dp")
    tensor = lax.axis_index("tensor")
    core = lax.rem(tensor, 2)
    other = 1 - core
    chip = tensor // 2
    x = chip // side
    y = lax.rem(chip, side)
    a = x * other + y * core
    b = y * other + x * core
    z_set = lax.rem(z, side)
    sign = 1 - 2 * core
    width = chips * LANES
    units = wk_hbm.shape[2]
    vocab_half = head_hbm.shape[2]
    rows = head_hbm.shape[1]
    slots = nz // 2
    near = {4: (1, -1, 2), 2: (1,)}[side]
    steps = (1, 3, 2) if side == 4 else (1,)
    ring = ((1, 0), (side - 1, 1)) if side == 4 else ((1, 0),)
    batches = BATCHES[nz]
    count = per_set * LANES

    def chip_at(at_a, at_b):
        return (at_a * side + at_b) * other + (at_b * side + at_a) * core

    def remote(src, dst, send, recv, to_z, to_chip, to_core):
        return pltpu.make_async_remote_copy(
            src_ref=src,
            dst_ref=dst,
            send_sem=send,
            recv_sem=recv,
            device_id={"dp": to_z, "tensor": to_chip * 2 + to_core},
            device_id_type=pl.DeviceIdType.MESH,
        )

    def await_bytes(view, sem):
        pltpu.make_async_copy(view, view, sem).wait()

    def wrap(value, size):
        return lax.rem(value + 4 * size, size)

    def lane(index):
        return pl.ds(pl.multiple_of(index * LANES, LANES), LANES)

    def pair_lane(index):
        return pl.ds(pl.multiple_of(index * 2 * LANES, 2 * LANES), 2 * LANES)

    def in_line(step):
        return chip_at(wrap(a + step, side), b)

    def across(step):
        return chip_at(a, wrap(b + step, side))

    unit_cols = pl.ds(pl.multiple_of(core * units, units), units)
    loads = (
        pltpu.make_async_copy(wk_hbm.at[core], wk_all.at[:, unit_cols], load_sem.at[0]),
        pltpu.make_async_copy(wv_hbm.at[core], wv_all.at[unit_cols, :], load_sem.at[1]),
        pltpu.make_async_copy(head_hbm.at[core], head_src.at[core], load_sem.at[2]),
    )
    small = (
        pltpu.make_async_copy(pages_hbm, pages_ref, load_sem.at[6]),
        pltpu.make_async_copy(mix_hbm, mix_ref, load_sem.at[7]),
        pltpu.make_async_copy(target_hbm, targets_all.at[z], load_sem.at[8]),
        pltpu.make_async_copy(gain_hbm, gain_ref, load_sem.at[9]),
        pltpu.make_async_copy(bias_hbm, bias_ref, load_sem.at[10]),
        pltpu.make_async_copy(table_hbm, table_ref, load_sem.at[11]),
        pltpu.make_async_copy(count_hbm, count_ref, load_sem.at[12]),
        pltpu.make_async_copy(last_hbm, last_ref, load_sem.at[13]),
    )
    for load in small + loads:
        load.start()

    barrier = pltpu.get_barrier_semaphore()

    def hello(to_z, to_chip, to_core):
        pl.semaphore_signal(
            barrier,
            inc=1,
            device_id={"dp": to_z, "tensor": to_chip * 2 + to_core},
            device_id_type=pl.DeviceIdType.MESH,
        )

    hello(z, chip, other)

    def hello_z(step, carry):
        hello(wrap(z + step, nz), chip, core)
        return carry

    def hello_plane(step, carry):
        hello(z, wrap(chip + step, chips), core)
        hello(z, wrap(chip + step, chips), other)
        return carry

    lax.fori_loop(1, nz, hello_z, 0)
    lax.fori_loop(1, chips, hello_plane, 0)
    for load in small:
        load.wait()
    pl.semaphore_wait(barrier, nz - 1 + 2 * (chips - 1) + 1)

    pair = (
        remote(pages_ref.at[other], pages_in, pair_send.at[0], pair_recv.at[0], z, chip, other),
        remote(mix_ref, mix_in, pair_send.at[1], pair_recv.at[1], z, chip, other),
        remote(
            head_hbm.at[other], head_src.at[core], pair_send.at[2], pair_recv.at[2], z, chip, other
        ),
        remote(
            wk_hbm.at[other],
            wk_all.at[:, unit_cols],
            pair_send.at[3],
            pair_recv.at[3],
            z,
            chip,
            other,
        ),
        remote(
            wv_hbm.at[other],
            wv_all.at[unit_cols, :],
            pair_send.at[4],
            pair_recv.at[4],
            z,
            chip,
            other,
        ),
    )
    for copy in pair:
        copy.start()

    pair[0].wait_recv()
    ours = pages_ref[core]
    theirs = pages_in[...]

    @pl.when(core == 0)
    def _():
        window[pl.ds(4, 4)] = jnp.concatenate([ours, theirs], axis=-1)

    @pl.when(core == 1)
    def _():
        window[pl.ds(4, 4)] = jnp.concatenate([theirs, ours], axis=-1)

    window_offsets = {4: (-1, 0, 1, 2), 2: (-1, 0)}[side]
    mine = window.at[pl.ds(4, 4)]
    moves = []
    for slot, offset in enumerate(window_offsets):
        if offset == 0:
            continue
        copy = remote(
            mine,
            window.at[pl.ds(slot * 4, 4)],
            win_send.at[slot],
            win_recv.at[slot],
            wrap(z - sign * offset, nz),
            chip,
            core,
        )
        copy.start()
        moves.append(copy)

    def head_row(index):
        place = (lax.rem(index, side) * side + index // side) * other + index * core
        return pl.ds(pl.multiple_of(place * rows, rows), rows)

    def head_piece(to_z):
        return head_src.at[to_z // slots, :, pair_lane(lax.rem(to_z, slots))]

    keep = pltpu.make_async_copy(
        head_piece(z), head_all.at[head_row(z), pair_lane(a)], load_sem.at[3]
    )

    def head_start(batch):
        for step in batches[batch]:
            if step == 0:
                keep.start()
                continue
            remote(
                head_piece(wrap(z + step, nz)),
                head_all.at[head_row(z), pair_lane(a)],
                hz_send,
                hz_recv.at[batch],
                wrap(z + step, nz),
                chip,
                core,
            ).start()

    def head_forward(batch):
        steps_in = batches[batch]
        if 0 in steps_in:
            keep.wait()
        arrived = len(steps_in) - (0 in steps_in)
        await_bytes(head_all.at[0 : arrived * rows, pair_lane(a)], hz_recv.at[batch])
        for step in steps_in:
            block = head_all.at[head_row(wrap(z - step, nz)), pair_lane(a)]
            for place, slot in ring:
                remote(
                    block, block, hf_send.at[slot], hf_recv.at[slot, batch], z, in_line(place), core
                ).start()

    def head_relay(batch):
        steps_in = batches[batch]
        for place, slot in ring:
            await_bytes(
                head_all.at[0 : len(steps_in) * rows, pair_lane(0)], hf_recv.at[slot, batch]
            )
        if side < 4:
            return
        for index, step in enumerate(steps_in):
            place, slot = ring[index % 2]
            source = wrap(a - place, side)
            block = head_all.at[head_row(wrap(z - step, nz)), pair_lane(source)]
            remote(
                block, block, hr_send, hr_recv.at[slot, batch], z, in_line(place), core
            ).start()

    for copy in moves:
        copy.wait_recv()

    picks = []
    for step in range(per_set):
        to_z = wrap(z + side * step, nz)
        for page in range(2):
            entry = table_ref[page, to_z]
            slot = lax.rem((entry // 4 - z) * sign + 1 + 4 * nz, nz)
            wanted = jnp.logical_and(slot < side, page < count_ref[to_z])
            flag = jnp.where(wanted, 1.0, 0.0).astype(F32)
            index = jnp.minimum(slot, side - 1) * 4 + lax.rem(entry, 4)
            block = (window[index].astype(F32) * flag).astype(BF16)
            if step == 0:
                picked[0, page] = block
            else:
                chosen[step, page] = block
        if step > 0:
            copy = remote(
                chosen.at[step],
                picked.at[step],
                pick_send.at[step],
                pick_recv.at[step],
                to_z,
                chip,
                core,
            )
            copy.start()
            picks.append(copy)

    loads[2].wait()
    pair[2].wait_recv()
    head_start(0)

    def send_target(step, carry):
        remote(
            targets_all.at[z],
            targets_all.at[z],
            tgt_send,
            tgt_recv,
            wrap(z + step, nz),
            chip,
            core,
        ).start()
        return carry

    lax.fori_loop(1, nz, send_target, 0)

    pair[1].wait_recv()
    for copy in picks:
        copy.wait_recv()
    state = picked[0].astype(F32)
    for step in range(1, per_set):
        state = state + picked[step].astype(F32)
    state = state.reshape(LANES, LANES)
    rolled = pltpu.roll(state, 1, 0)
    previous = jnp.where(iota((LANES, LANES), 0) == 0, 0.0, rolled)
    model = core.astype(F32)

    def of_model(pair_rows):
        return pair_rows[0:1] * (1.0 - model) + pair_rows[1:2] * model

    ours = of_model(mix_ref[...])
    theirs = of_model(mix_in[...])
    low = jnp.concatenate([ours, theirs], axis=-1)
    high = jnp.concatenate([theirs, ours], axis=-1)
    mix = low * (1.0 - model) + high * model
    shift_blocks[b, a] = (state + (previous - state) * mix).astype(BF16)

    line = []
    for index, step in enumerate(steps):
        block = shift_blocks.at[b, a]
        copy = remote(block, block, sa_send.at[index], sa_recv.at[index], z, in_line(step), core)
        copy.start()
        line.append(copy)
    head_start(1)
    for copy in line:
        copy.wait_recv()
    cross = []
    for index, step in enumerate(steps):
        block = shift_blocks.at[b]
        copy = remote(block, block, sb_send.at[index], sb_recv.at[index], z, across(step), core)
        copy.start()
        cross.append(copy)
    loads[0].wait()
    loads[1].wait()
    pair[3].wait_recv()
    pair[4].wait_recv()
    for copy in cross:
        copy.wait_recv()
    for at_b in range(side):
        for at_a in range(side):
            shifted_all[:, lane(chip_at(at_a, at_b))] = shift_blocks[at_b, at_a]

    hidden = jnp.dot(shifted_all[...], wk_all[...], preferred_element_type=F32)
    act[...] = (jnp.maximum(hidden, 0.0) ** 2).astype(BF16)
    sums = []
    for index, step in enumerate((side // 2,) + tuple(s for s in steps if s != side // 2) + (0,)):
        to_a = wrap(a + step, side)

        def mix_out(to_b, carry):
            cols = lane(chip_at(to_a, to_b))
            partial[to_a, to_b] = jnp.dot(
                act[...], wv_all[:, cols], preferred_element_type=F32
            )
            return carry

        lax.fori_loop(0, side, mix_out, 0)
        if step:
            copy = remote(
                partial.at[to_a],
                line_sums.at[step],
                ra_send.at[step],
                ra_recv.at[step],
                z,
                in_line(step),
                core,
            )
            copy.start()
            sums.append(copy)
    if len(batches) > 2:
        head_start(2)
    total = partial[a]
    for copy in sums:
        copy.wait_recv()
    for step in steps:
        total = total + line_sums[step]
    line_total[...] = total
    crosses = []
    for step in steps:
        copy = remote(
            line_total.at[wrap(b + step, side)],
            cross_sums.at[step],
            rb_send.at[step],
            rb_recv.at[step],
            z,
            across(step),
            core,
        )
        copy.start()
        crosses.append(copy)
    if len(batches) > 2:
        head_start(3)
    residual = state + line_total[b]
    for step, copy in zip(steps, crosses):
        copy.wait_recv()
    for step in steps:
        residual = residual + cross_sums[step]

    turned = residual.T
    stats[chip] = rows_of(
        jnp.sum(turned, axis=0, keepdims=True), jnp.sum(turned * turned, axis=0, keepdims=True)
    )

    def stat_start(step, carry):
        remote(
            stats.at[chip],
            stats.at[chip],
            stat_send,
            stat_recv,
            z,
            wrap(chip + step, chips),
            core,
        ).start()
        return carry

    lax.fori_loop(1, chips, stat_start, 0)
    head_forward(0)
    await_bytes(stats.at[pl.ds(0, chips - 1)], stat_recv)
    total = jnp.sum(stats[...], axis=0)
    average = total[0:1] / width
    variance = total[1:2] / width - average * average
    scale = lax.rsqrt(variance + epsilon)
    gain = of_model(gain_ref[:, lane(chip)])
    bias = of_model(bias_ref[:, lane(chip)])
    normed = (residual - column_of(average)) * column_of(scale) * gain + bias
    place = z // side
    sets[0, place] = normed.astype(BF16)

    sends = []
    for step in range(1, per_set):
        copy = remote(
            sets.at[0, place],
            sets.at[0, place],
            set_send.at[step],
            set_recv.at[step],
            wrap(z + side * step, nz),
            chip,
            core,
        )
        copy.start()
        sends.append(copy)
    head_forward(1)
    head_relay(0)

    for copy in sends:
        copy.wait_recv()
    nears = []
    for slot, offset in enumerate(near):
        copy = remote(
            sets.at[0],
            sets.at[slot + 1],
            near_send.at[slot],
            near_recv.at[slot],
            wrap(z - sign * offset, nz),
            chip,
            core,
        )
        copy.start()
        nears.append(copy)

    def token_cols(at_b, at_a):
        return lane(at_b * side + at_a)

    for slot in range(side):
        if slot > 0:
            nears[slot - 1].wait_recv()
        offset = 0 if slot == 0 else near[slot - 1]
        group = lax.rem(wrap(z + sign * offset, nz), side)

        @pl.when(group == a)
        def _():
            tokens[:, :, token_cols(b, a)] = sets[slot]

        @pl.when(group != a)
        def _():
            remote(
                sets.at[slot],
                tokens.at[:, :, token_cols(b, a)],
                ta_send,
                ta_recv,
                z,
                chip_at(group, b),
                core,
            ).start()

        if slot == 0:
            if len(batches) > 2:
                head_forward(2)
            head_relay(1)

    await_bytes(targets_all.at[pl.ds(0, nz - 1)], tgt_recv)
    wanted = jnp.concatenate(
        [
            column_of(targets_all[a + side * step].astype(F32))
            for step in range(per_set)
        ],
        axis=0,
    )

    if len(batches) > 2:
        head_forward(3)
        head_relay(2)

    def token_block(at_b, first, size):
        start = pl.multiple_of((at_b * side + first) * LANES, LANES)
        return tokens.at[:, :, pl.ds(start, size * LANES)]

    await_bytes(tokens.at[:, :, pl.ds(0, (side - 1) * LANES)], ta_recv)
    for place, slot in ring:
        block = token_block(b, 0, side)
        remote(block, block, tb_send.at[slot], tb_recv.at[slot], z, across(place), core).start()
    if len(batches) > 2:
        head_relay(3)
    for place, slot in ring:
        await_bytes(token_block(0, 0, side), tb_recv.at[slot])
        if side == 4:
            block = token_block(wrap(b - place, side), 2 * slot, 2)
            remote(block, block, tr_send, tr_recv.at[slot], z, across(place), core).start()
    if side == 4:
        for place, slot in ring:
            for batch, steps_in in enumerate(batches):
                await_bytes(
                    head_all.at[0 : len(steps_in) // 2 * rows, pair_lane(0)],
                    hr_recv.at[slot, batch],
                )
        for place, slot in ring:
            await_bytes(token_block(0, 0, 2), tr_recv.at[slot])

    def make_logits(block, peak):
        part = jnp.dot(
            tokens[...].reshape(count, width),
            head_all[:, pair_lane(block)],
            preferred_element_type=F32,
        )
        logits[block] = part
        return jnp.maximum(peak, jnp.maximum(part[:, :LANES], part[:, LANES:]))

    peak = lax.fori_loop(0, side, make_logits, jnp.full((count, LANES), -jnp.inf, F32))
    peak = jnp.max(peak, axis=1, keepdims=True)
    total = jnp.zeros((count, LANES), F32)
    hit = jnp.zeros((count, LANES), F32)
    column = iota((count, LANES), 1).astype(F32)
    for block in range(side):
        for half in range(2):
            part = logits[block, :, half * LANES : (half + 1) * LANES]
            total = total + jnp.exp(part - peak)
            base = chip_at(block, b) * 2 * vocab_half + (z * 2 + half) * LANES
            hit = hit + jnp.where(wanted - base.astype(F32) == column, part, 0.0)
    total = jnp.sum(total, axis=1, keepdims=True)
    hit = jnp.sum(hit, axis=1, keepdims=True)
    column = iota((count, LANES), 1)
    packed = jnp.where(column == 0, peak, jnp.where(column == 1, total, hit))
    for step in range(per_set):
        turned = packed[step * LANES : (step + 1) * LANES].T
        local_stats[step] = turned[0:8]

    for step in range(per_set):
        to_z = a + side * step

        @pl.when(to_z == z)
        def _():
            column_stats[z] = local_stats[step]

        @pl.when(to_z != z)
        def _():
            remote(
                local_stats.at[step], column_stats.at[z], c0_send.at[step], c0_recv, to_z, chip, core
            ).start()

    def combine(parts):
        peaks = parts[:, 0:1, :]
        top = jnp.max(peaks, axis=0)
        sums = jnp.sum(parts[:, 1:2, :] * jnp.exp(peaks - top[None]), axis=0)
        return top, sums, jnp.sum(parts[:, 2:3, :], axis=0)

    mine = plane_stats.at[core, b]

    @pl.when(a == z_set)
    def _():
        await_bytes(column_stats.at[pl.ds(0, nz - 1)], c0_recv)
        plane_stats[core, b] = rows_of(*combine(column_stats[...]))

        def plane_start(step, carry):
            to_chip = wrap(chip + step, chips)
            remote(mine, mine, c1_send.at[0], c1_recv.at[core, b], z, to_chip, core).start()
            remote(mine, mine, c1_send.at[1], c1_recv.at[core, b], z, to_chip, other).start()
            return carry

        remote(mine, mine, c1_send.at[1], c1_recv.at[core, b], z, chip, other).start()
        lax.fori_loop(1, chips, plane_start, 0)

    for of_core in range(2):
        for at_b in range(side):
            theirs = plane_stats.at[of_core, at_b]
            ours = jnp.logical_and(
                jnp.logical_and(core == of_core, b == at_b), a == z_set
            )

            @pl.when(jnp.logical_not(ours))
            def _():
                await_bytes(theirs, c1_recv.at[of_core, at_b])

    logp = []
    for of_core in range(2):
        top, sums_all, hits = combine(plane_stats[of_core])
        logp.append(hits - top - jnp.log(sums_all))
    length = (count_ref[z] - 1) * 64 + last_ref[z]
    valid = iota((1, LANES), 1) < length
    row = jnp.where(valid, logp[0], 0.0)
    ratio_out[...] = jnp.sum(
        jnp.where(valid, logp[0] - logp[1], 0.0), axis=1, keepdims=True
    )
    share = token_out.shape[1]
    row = pltpu.roll(jnp.broadcast_to(row, (8, LANES)), lax.rem(LANES - tensor * share, LANES), 1)
    token_out[...] = row[0:1, 0:share]

    for copy in pair:
        copy.wait_send()
    for copy in moves + picks + line + cross + sums + crosses + sends + nears:
        copy.wait_send()
    await_bytes(targets_all.at[pl.ds(0, nz - 1)], tgt_send)
    await_bytes(stats.at[pl.ds(0, chips - 1)], stat_send)
    await_bytes(head_all.at[0 : (nz - 1) * rows, pair_lane(0)], hz_send)
    for place, slot in ring:
        await_bytes(head_all.at[:, pair_lane(0)], hf_send.at[slot])
        await_bytes(token_block(0, 0, side), tb_send.at[slot])
    await_bytes(tokens.at[:, :, pl.ds(0, (side - 1) * LANES)], ta_send)
    if side == 4:
        await_bytes(head_all.at[:, pair_lane(0)], hr_send)
        await_bytes(token_block(0, 0, side), tr_send)
    for step in range(per_set):

        @pl.when(a + side * step != z)
        def _():
            await_bytes(local_stats.at[step], c0_send.at[step])

    @pl.when(a == z_set)
    def _():
        await_bytes(stats.at[pl.ds(0, chips - 1)], c1_send.at[0])
        await_bytes(stats, c1_send.at[1])


def body(
    nz,
    side,
    pages,
    page_table,
    page_count,
    last_len,
    targets,
    mix_key,
    w_key,
    w_value,
    ln_gain,
    ln_bias,
    head,
):
    chips = side * side
    per_set = nz // side
    width = chips * LANES
    units = w_key.shape[2]
    rows = head.shape[1]
    vmem = pl.BlockSpec(memory_space=pltpu.VMEM)
    hbm = pl.BlockSpec(memory_space=pl.ANY)
    dma = pltpu.SemaphoreType.DMA
    batches = len(BATCHES[nz])
    share = LANES // (2 * chips)
    semaphores = [6, 6, 14, (), ()]
    semaphores += [4] * 2 + [per_set] * 2 + [side] * 8
    semaphores += [(), (), (), batches, 2, (2, batches), (), (2, batches)]
    semaphores += [per_set] * 2 + [side] * 2 + [(), (), 2, 2, (), 2]
    semaphores += [per_set, (), 2, (2, side)]
    result = pl.pallas_call(
        functools.partial(kernel, nz, side),
        out_shape=(
            jax.ShapeDtypeStruct((1, share), F32),
            jax.ShapeDtypeStruct((1, 1), F32),
        ),
        in_specs=[hbm] * 11,
        out_specs=(vmem, vmem),
        scratch_shapes=[
            pltpu.SMEM(page_table.shape[::-1], jnp.int32),
            pltpu.SMEM(page_count.shape, jnp.int32),
            pltpu.SMEM(last_len.shape, jnp.int32),
            pltpu.VMEM(pages.shape, BF16),
            pltpu.VMEM(mix_key.shape, F32),
            pltpu.VMEM(ln_gain.shape, F32),
            pltpu.VMEM(ln_bias.shape, F32),
            pltpu.VMEM(pages.shape[1:], BF16),
            pltpu.VMEM(mix_key.shape, F32),
            pltpu.VMEM((nz, 1, LANES), jnp.int32),
            pltpu.VMEM((2, rows, head.shape[2]), BF16),
            pltpu.VMEM((width, 2 * side * LANES), BF16),
            pltpu.VMEM((width, 2 * units), BF16),
            pltpu.VMEM((2 * units, width), BF16),
            pltpu.VMEM((side * 4, 64, LANES), BF16),
            pltpu.VMEM((per_set, 2, 64, LANES), BF16),
            pltpu.VMEM((per_set, 2, 64, LANES), BF16),
            pltpu.VMEM((side, side, LANES, LANES), BF16),
            pltpu.VMEM((LANES, width), BF16),
            pltpu.VMEM((LANES, 2 * units), BF16),
            pltpu.VMEM((side, side, LANES, LANES), F32),
            pltpu.VMEM((side, side, LANES, LANES), F32),
            pltpu.VMEM((side, LANES, LANES), F32),
            pltpu.VMEM((side, LANES, LANES), F32),
            pltpu.VMEM((chips, 8, LANES), F32),
            pltpu.VMEM((side, per_set, LANES, LANES), BF16),
            pltpu.VMEM((per_set, LANES, width), BF16),
            pltpu.VMEM((side, per_set * LANES, 2 * LANES), F32),
            pltpu.VMEM((per_set, 8, LANES), F32),
            pltpu.VMEM((nz, 8, LANES), F32),
            pltpu.VMEM((2, side, 8, LANES), F32),
        ]
        + [dma(size if isinstance(size, tuple) else (size,)) for size in semaphores],
        compiler_params=pltpu.CompilerParams(
            collective_id=0, has_side_effects=True, vmem_limit_bytes=VMEM_LIMIT
        ),
    )(
        page_table.T,
        page_count,
        last_len,
        pages,
        mix_key,
        targets,
        ln_gain,
        ln_bias,
        w_key,
        w_value,
        head,
    )
    token_part, ratio = result
    return token_part, ratio.reshape(1)


def solution(mesh):
    nz = mesh.shape["dp"]
    side = {32: 4, 8: 2}[mesh.shape["tensor"]]
    specs = (
        P(None, "dp", None, "tensor"),
        P(),
        P(),
        P(),
        P("dp", None),
        P(None, "tensor"),
        P(None, None, "tensor"),
        P(None, "tensor", None),
        P(),
        P(),
        P(None, "dp", "tensor"),
    )
    return jax.shard_map(
        functools.partial(body, nz, side),
        mesh=mesh,
        in_specs=specs,
        out_specs=(P("dp", "tensor"), P("dp")),
        check_vma=False,
    )
```

time: 173 us -> 138 us (0.80)
  Pallas kernels: 160 us -> 134 us
  local copies, waits for them, and re-layouts: 9.66 us -> 1.11 us
  other arithmetic: 1.8 us -> 0 us
  between operations: 0.67 us -> 2.41 us
    pallas_call x1, Pallas kernels: 160 us -> 134 us  [body(): pl.pallas_call(functools.partial(kernel, nz, side), out_shape=(jax.ShapeD...]
    unnamed x15 -> x1, local copies, waits for them, and re-layouts: 7.9 us -> 1.11 us
where the time goes in v2:
time: 138 us
  Pallas kernels  134 us (97%)
  between operations  2.41 us (2%)
    pallas_call x1, Pallas kernels, body(): pl.pallas_call(functools.partial(kernel, nz, side), out_shape=(jax.ShapeD...  134 us

profile of v2, /device:TPU:1, one launch (start us, length us, event | category | flops | bytes accessed | tf_op | source)
XLA Modules:
  0.0 137.5 jit_solution(12568100808717796329)
XLA Ops:
  0.6 134.0 %shard_map.122 = (f32[1,4]{1,0:T(1,128)}, f32[1,1]{1,0:T(1,128)}) custom-call(s32[2,16]{1,0:T(2,128)} %bitcast.2, s32[16]{0:T(128)} %count_hbm.1, s32[16]{0:T(128)} %last_hbm.1, bf16[2,4,64,64]{3,2,1,0:T(8,128)(2,1)} %pages_hbm.1, f32[2,64]{1,0:T(2,128)} %mix_hbm.1, s32[1,128]{1,0:T(1,128)} %target_hbm.1, f32[2,2048]{1,0:T(2,128)} %gain_hbm.1, ...), custom_call_target="tpu_custom_call" | custom-call | tf_op jit(solution)/shard_map/pallas_call | solution.py:758
  134.6 1.1 copy.15

commit v3 on v2

--- a/solution.py
+++ b/solution.py
@@ -13,6 +13,20 @@
 LANES = 128
 BATCHES = {16: ((0, 8, 4, 12), (1, 15, 7, 9), (2, 14, 6, 10), (3, 13, 5, 11)), 4: ((0, 2), (1, 3))}
 VMEM_LIMIT = 63 * 1024 * 1024
+
+
+ORDER = {4: (0, 1, 3, 2), 2: (0, 1)}
+PARTS = {4: ((0, 3, (1, 3)), (3, 1, (2,))), 2: ((0, 1, ()), (1, 1, (1,)))}
+SCHEDULE = {
+    1: (("s", 0), ("s", 1)),
+    2: (("s", 2),),
+    4: (("s", 3),),
+    5: (("f", 0),),
+    6: (("f", 1), ("r", 0)),
+    7: (("f", 2), ("r", 1)),
+    9: (("f", 3), ("r", 2)),
+    10: (("r", 3),),
+}
 
 
 def iota(shape, axis):
@@ -45,8 +59,7 @@
     wk_hbm,
     wv_hbm,
     head_hbm,
-    token_out,
-    ratio_out,
+    out_ref,
     table_ref,
     count_ref,
     last_ref,
@@ -105,8 +118,6 @@
     hr_recv,
     set_send,
     set_recv,
-    near_send,
-    near_recv,
     ta_send,
     ta_recv,
     tb_send,
@@ -141,6 +152,18 @@
     ring = ((1, 0), (side - 1, 1)) if side == 4 else ((1, 0),)
     batches = BATCHES[nz]
     count = per_set * LANES
+    order = ORDER[per_set]
+    parts = PARTS[per_set]
+
+    def wrap(value, size):
+        return lax.rem(value + 4 * size, size)
+
+    gap = wrap(a - z_set, side)
+    if side == 4:
+        gap = gap - 4 * (gap // 3) + 2 * (sign - 1) * (gap // 2 - gap // 3)
+    else:
+        gap = gap * sign
+    from_z = wrap(z + gap, nz)
 
     def chip_at(at_a, at_b):
         return (at_a * side + at_b) * other + (at_b * side + at_a) * core
@@ -157,9 +180,6 @@
 
     def await_bytes(view, sem):
         pltpu.make_async_copy(view, view, sem).wait()
-
-    def wrap(value, size):
-        return lax.rem(value + 4 * size, size)
 
     def lane(index):
         return pl.ds(pl.multiple_of(index * LANES, LANES), LANES)
@@ -213,11 +233,16 @@
         hello(z, wrap(chip + step, chips), other)
         return carry
 
+    @pl.when(gap != 0)
+    def _():
+        for at_a in range(side):
+            hello(from_z, chip_at(at_a, b), core)
+
     lax.fori_loop(1, nz, hello_z, 0)
     lax.fori_loop(1, chips, hello_plane, 0)
     for load in small:
         load.wait()
-    pl.semaphore_wait(barrier, nz - 1 + 2 * (chips - 1) + 1)
+    pl.semaphore_wait(barrier, nz - 1 + 2 * (chips - 1) + 1 + len(near))
 
     pair = (
         remote(pages_ref.at[other], pages_in, pair_send.at[0], pair_recv.at[0], z, chip, other),
@@ -247,6 +272,70 @@
     for copy in pair:
         copy.start()
 
+    def head_row(index):
+        place = (lax.rem(index, side) * side + index // side) * other + index * core
+        return pl.ds(pl.multiple_of(place * rows, rows), rows)
+
+    def head_piece(to_z):
+        return head_src.at[to_z // slots, :, pair_lane(lax.rem(to_z, slots))]
+
+    keep = pltpu.make_async_copy(
+        head_piece(z), head_all.at[head_row(z), pair_lane(a)], load_sem.at[3]
+    )
+
+    def head_start(batch):
+        for step in batches[batch]:
+            if step == 0:
+                keep.start()
+                continue
+            remote(
+                head_piece(wrap(z + step, nz)),
+                head_all.at[head_row(z), pair_lane(a)],
+                hz_send,
+                hz_recv.at[batch],
+                wrap(z + step, nz),
+                chip,
+                core,
+            ).start()
+
+    def head_forward(batch):
+        steps_in = batches[batch]
+        if 0 in steps_in:
+            keep.wait()
+        arrived = len(steps_in) - (0 in steps_in)
+        await_bytes(head_all.at[0 : arrived * rows, pair_lane(a)], hz_recv.at[batch])
+        for step in steps_in:
+            block = head_all.at[head_row(wrap(z - step, nz)), pair_lane(a)]
+            for place, slot in ring:
+                remote(
+                    block, block, hf_send.at[slot], hf_recv.at[slot, batch], z, in_line(place), core
+                ).start()
+
+    def head_relay(batch):
+        steps_in = batches[batch]
+        for place, slot in ring:
+            await_bytes(
+                head_all.at[0 : len(steps_in) * rows, pair_lane(0)], hf_recv.at[slot, batch]
+            )
+        if side < 4:
+            return
+        for index, step in enumerate(steps_in):
+            place, slot = ring[index % 2]
+            source = wrap(a - place, side)
+            block = head_all.at[head_row(wrap(z - step, nz)), pair_lane(source)]
+            remote(
+                block, block, hr_send, hr_recv.at[slot, batch], z, in_line(place), core
+            ).start()
+
+    def at(point):
+        for action, batch in SCHEDULE.get(point, ()):
+            if batch >= len(batches):
+                continue
+            if (action, batch) == ("s", 0):
+                loads[2].wait()
+                pair[2].wait_recv()
+            {"s": head_start, "f": head_forward, "r": head_relay}[action](batch)
+
     pair[0].wait_recv()
     ours = pages_ref[core]
     theirs = pages_in[...]
@@ -277,61 +366,7 @@
         copy.start()
         moves.append(copy)
 
-    def head_row(index):
-        place = (lax.rem(index, side) * side + index // side) * other + index * core
-        return pl.ds(pl.multiple_of(place * rows, rows), rows)
-
-    def head_piece(to_z):
-        return head_src.at[to_z // slots, :, pair_lane(lax.rem(to_z, slots))]
-
-    keep = pltpu.make_async_copy(
-        head_piece(z), head_all.at[head_row(z), pair_lane(a)], load_sem.at[3]
-    )
-
-    def head_start(batch):
-        for step in batches[batch]:
-            if step == 0:
-                keep.start()
-                continue
-            remote(
-                head_piece(wrap(z + step, nz)),
-                head_all.at[head_row(z), pair_lane(a)],
-                hz_send,
-                hz_recv.at[batch],
-                wrap(z + step, nz),
-                chip,
-                core,
-            ).start()
-
-    def head_forward(batch):
-        steps_in = batches[batch]
-        if 0 in steps_in:
-            keep.wait()
-        arrived = len(steps_in) - (0 in steps_in)
-        await_bytes(head_all.at[0 : arrived * rows, pair_lane(a)], hz_recv.at[batch])
-        for step in steps_in:
-            block = head_all.at[head_row(wrap(z - step, nz)), pair_lane(a)]
-            for place, slot in ring:
-                remote(
-                    block, block, hf_send.at[slot], hf_recv.at[slot, batch], z, in_line(place), core
-                ).start()
-
-    def head_relay(batch):
-        steps_in = batches[batch]
-        for place, slot in ring:
-            await_bytes(
-                head_all.at[0 : len(steps_in) * rows, pair_lane(0)], hf_recv.at[slot, batch]
-            )
-        if side < 4:
-            return
-        for index, step in enumerate(steps_in):
-            place, slot = ring[index % 2]
-            source = wrap(a - place, side)
-            block = head_all.at[head_row(wrap(z - step, nz)), pair_lane(source)]
-            remote(
-                block, block, hr_send, hr_recv.at[slot, batch], z, in_line(place), core
-            ).start()
-
+    at(0)
     for copy in moves:
         copy.wait_recv()
 
@@ -362,9 +397,7 @@
             copy.start()
             picks.append(copy)
 
-    loads[2].wait()
-    pair[2].wait_recv()
-    head_start(0)
+    at(1)
 
     def send_target(step, carry):
         remote(
@@ -407,7 +440,7 @@
         copy = remote(block, block, sa_send.at[index], sa_recv.at[index], z, in_line(step), core)
         copy.start()
         line.append(copy)
-    head_start(1)
+    at(2)
     for copy in line:
         copy.wait_recv()
     cross = []
@@ -416,6 +449,7 @@
         copy = remote(block, block, sb_send.at[index], sb_recv.at[index], z, across(step), core)
         copy.start()
         cross.append(copy)
+    at(3)
     loads[0].wait()
     loads[1].wait()
     pair[3].wait_recv()
@@ -452,8 +486,7 @@
             )
             copy.start()
             sums.append(copy)
-    if len(batches) > 2:
-        head_start(2)
+    at(4)
     total = partial[a]
     for copy in sums:
         copy.wait_recv()
@@ -473,8 +506,7 @@
         )
         copy.start()
         crosses.append(copy)
-    if len(batches) > 2:
-        head_start(3)
+    at(5)
     residual = state + line_total[b]
     for step, copy in zip(steps, crosses):
         copy.wait_recv()
@@ -499,7 +531,7 @@
         return carry
 
     lax.fori_loop(1, chips, stat_start, 0)
-    head_forward(0)
+    at(6)
     await_bytes(stats.at[pl.ds(0, chips - 1)], stat_recv)
     total = jnp.sum(stats[...], axis=0)
     average = total[0:1] / width
@@ -508,99 +540,91 @@
     gain = of_model(gain_ref[:, lane(chip)])
     bias = of_model(bias_ref[:, lane(chip)])
     normed = (residual - column_of(average)) * column_of(scale) * gain + bias
-    place = z // side
-    sets[0, place] = normed.astype(BF16)
-
-    sends = []
+    sets[0] = normed.astype(BF16)
+
+    sends = {}
     for step in range(1, per_set):
-        copy = remote(
-            sets.at[0, place],
-            sets.at[0, place],
+        slot = order.index(per_set - step)
+        sends[step] = remote(
+            sets.at[0],
+            sets.at[slot],
             set_send.at[step],
             set_recv.at[step],
             wrap(z + side * step, nz),
             chip,
             core,
         )
-        copy.start()
-        sends.append(copy)
-    head_forward(1)
-    head_relay(0)
-
-    for copy in sends:
-        copy.wait_recv()
-    nears = []
-    for slot, offset in enumerate(near):
-        copy = remote(
-            sets.at[0],
-            sets.at[slot + 1],
-            near_send.at[slot],
-            near_recv.at[slot],
-            wrap(z - sign * offset, nz),
-            chip,
+        sends[step].start()
+    at(7)
+
+    def token_cols(at_b, at_a):
+        return lane(at_b * side + at_a)
+
+    def token_copy(first, size, at_a, to_z):
+        return remote(
+            sets.at[pl.ds(first, size)],
+            tokens.at[pl.ds(first, size), :, token_cols(b, at_a)],
+            ta_send,
+            ta_recv.at[at_a],
+            to_z,
+            chip_at(z_set, b),
             core,
         )
-        copy.start()
-        nears.append(copy)
-
-    def token_cols(at_b, at_a):
-        return lane(at_b * side + at_a)
-
-    for slot in range(side):
-        if slot > 0:
-            nears[slot - 1].wait_recv()
-        offset = 0 if slot == 0 else near[slot - 1]
-        group = lax.rem(wrap(z + sign * offset, nz), side)
-
-        @pl.when(group == a)
-        def _():
-            tokens[:, :, token_cols(b, a)] = sets[slot]
-
-        @pl.when(group != a)
-        def _():
-            remote(
-                sets.at[slot],
-                tokens.at[:, :, token_cols(b, a)],
-                ta_send,
-                ta_recv,
-                z,
-                chip_at(group, b),
-                core,
-            ).start()
-
-        if slot == 0:
-            if len(batches) > 2:
-                head_forward(2)
-            head_relay(1)
+
+    for index, (first, size, needs) in enumerate(parts):
+        for step in needs:
+            sends[step].wait_recv()
+        for offset in reversed((0,) + near):
+            if offset:
+                token_copy(first, size, a, wrap(z - sign * offset, nz)).start()
+                continue
+
+            @pl.when(gap == 0)
+            def _():
+                tokens[first : first + size, :, token_cols(b, a)] = sets[first : first + size]
+
+            @pl.when(gap != 0)
+            def _():
+                token_copy(first, size, a, z).start()
+
+        at(8 + index)
 
     await_bytes(targets_all.at[pl.ds(0, nz - 1)], tgt_recv)
+    rollouts = [wrap(from_z + side * step, nz) for step in order]
     wanted = jnp.concatenate(
-        [
-            column_of(targets_all[a + side * step].astype(F32))
-            for step in range(per_set)
-        ],
-        axis=0,
+        [column_of(targets_all[rollout].astype(F32)) for rollout in rollouts], axis=0
     )
 
-    if len(batches) > 2:
-        head_forward(3)
-        head_relay(2)
+    half = side // 2
 
     def token_block(at_b, first, size):
         start = pl.multiple_of((at_b * side + first) * LANES, LANES)
         return tokens.at[:, :, pl.ds(start, size * LANES)]
 
-    await_bytes(tokens.at[:, :, pl.ds(0, (side - 1) * LANES)], ta_recv)
+    for at_a in range(side):
+
+        @pl.when(jnp.logical_not(jnp.logical_and(gap == 0, a == at_a)))
+        def _():
+            await_bytes(tokens.at[:, :, pl.ds(0, LANES)], ta_recv.at[at_a])
+
+    for turn in range(2):
+        for place, slot in ring:
+            part = (turn + slot) % 2
+            block = token_block(b, part * half, half)
+            remote(
+                block, block, tb_send.at[slot], tb_recv.at[slot, turn], z, across(place), core
+            ).start()
+    at(10)
+    if side == 4:
+        for place, slot in ring:
+            await_bytes(token_block(0, 0, half), tb_recv.at[slot, 0])
+            block = token_block(wrap(b - place, side), slot * half, half)
+            remote(block, block, tr_send, tr_recv.at[slot], z, across(place), core).start()
+    else:
+        await_bytes(token_block(0, 0, half), tb_recv.at[0, 0])
+    at(11)
     for place, slot in ring:
-        block = token_block(b, 0, side)
-        remote(block, block, tb_send.at[slot], tb_recv.at[slot], z, across(place), core).start()
-    if len(batches) > 2:
-        head_relay(3)
-    for place, slot in ring:
-        await_bytes(token_block(0, 0, side), tb_recv.at[slot])
-        if side == 4:
-            block = token_block(wrap(b - place, side), 2 * slot, 2)
-            remote(block, block, tr_send, tr_recv.at[slot], z, across(place), core).start()
+        await_bytes(token_block(0, 0, half), tb_recv.at[slot, 1])
     if side == 4:
         for place, slot in ring:
             for batch, steps_in in enumerate(batches):
@@ -609,7 +633,7 @@
                     hr_recv.at[slot, batch],
                 )
         for place, slot in ring:
-            await_bytes(token_block(0, 0, 2), tr_recv.at[slot])
+            await_bytes(token_block(0, 0, half), tr_recv.at[slot])
 
     def make_logits(block, peak):
         part = jnp.dot(
@@ -640,7 +664,7 @@
         local_stats[step] = turned[0:8]
 
     for step in range(per_set):
-        to_z = a + side * step
+        to_z = rollouts[step]
 
         @pl.when(to_z == z)
         def _():
@@ -692,16 +716,12 @@
     length = (count_ref[z] - 1) * 64 + last_ref[z]
     valid = iota((1, LANES), 1) < length
     row = jnp.where(valid, logp[0], 0.0)
-    ratio_out[...] = jnp.sum(
-        jnp.where(valid, logp[0] - logp[1], 0.0), axis=1, keepdims=True
-    )
-    share = token_out.shape[1]
-    row = pltpu.roll(jnp.broadcast_to(row, (8, LANES)), lax.rem(LANES - tensor * share, LANES), 1)
-    token_out[...] = row[0:1, 0:share]
+    ratio = jnp.sum(jnp.where(valid, logp[0] - logp[1], 0.0), axis=1, keepdims=True)
+    out_ref[...] = rows_of(row, jnp.broadcast_to(ratio, (1, LANES)))
 
     for copy in pair:
         copy.wait_send()
-    for copy in moves + picks + line + cross + sums + crosses + sends + nears:
+    for copy in moves + picks + line + cross + sums + crosses + list(sends.values()):
         copy.wait_send()
     await_bytes(targets_all.at[pl.ds(0, nz - 1)], tgt_send)
     await_bytes(stats.at[pl.ds(0, chips - 1)], stat_send)
@@ -709,13 +729,22 @@
     for place, slot in ring:
         await_bytes(head_all.at[:, pair_lane(0)], hf_send.at[slot])
         await_bytes(token_block(0, 0, side), tb_send.at[slot])
-    await_bytes(tokens.at[:, :, pl.ds(0, (side - 1) * LANES)], ta_send)
+    sent = tokens.at[:, :, pl.ds(0, len(near) * LANES)]
+
+    @pl.when(gap == 0)
+    def _():
+        await_bytes(sent, ta_send)
+
+    @pl.when(gap != 0)
+    def _():
+        await_bytes(tokens.at[:, :, pl.ds(0, side * LANES)], ta_send)
+
     if side == 4:
         await_bytes(head_all.at[:, pair_lane(0)], hr_send)
         await_bytes(token_block(0, 0, side), tr_send)
     for step in range(per_set):
 
-        @pl.when(a + side * step != z)
+        @pl.when(rollouts[step] != z)
         def _():
             await_bytes(local_stats.at[step], c0_send.at[step])
 
@@ -753,16 +782,13 @@
     semaphores = [6, 6, 14, (), ()]
     semaphores += [4] * 2 + [per_set] * 2 + [side] * 8
     semaphores += [(), (), (), batches, 2, (2, batches), (), (2, batches)]
-    semaphores += [per_set] * 2 + [side] * 2 + [(), (), 2, 2, (), 2]
+    semaphores += [per_set] * 2 + [(), side, 2, (2, 2), (), 2]
     semaphores += [per_set, (), 2, (2, side)]
     result = pl.pallas_call(
         functools.partial(kernel, nz, side),
-        out_shape=(
-            jax.ShapeDtypeStruct((1, share), F32),
-            jax.ShapeDtypeStruct((1, 1), F32),
-        ),
+        out_shape=jax.ShapeDtypeStruct((8, LANES), F32),
         in_specs=[hbm] * 11,
-        out_specs=(vmem, vmem),
+        out_specs=vmem,
         scratch_shapes=[
             pltpu.SMEM(page_table.shape[::-1], jnp.int32),
             pltpu.SMEM(page_count.shape, jnp.int32),
@@ -789,7 +815,7 @@
             pltpu.VMEM((side, LANES, LANES), F32),
             pltpu.VMEM((side, LANES, LANES), F32),
             pltpu.VMEM((chips, 8, LANES), F32),
-            pltpu.VMEM((side, per_set, LANES, LANES), BF16),
+            pltpu.VMEM((per_set, LANES, LANES), BF16),
             pltpu.VMEM((per_set, LANES, width), BF16),
             pltpu.VMEM((side, per_set * LANES, 2 * LANES), F32),
             pltpu.VMEM((per_set, 8, LANES), F32),
@@ -813,8 +839,8 @@
         w_value,
         head,
     )
-    token_part, ratio = result
-    return token_part, ratio.reshape(1)
+    start = lax.axis_index("tensor") * share
+    return lax.dynamic_slice(result, (0, start), (1, share)), result[1, 0:1]
 
 
 def solution(mesh):

time: 138 us -> 123 us (0.89)
  Pallas kernels: 134 us -> 119 us
  between operations: 2.41 us -> 0.65 us
    pallas_call x1, Pallas kernels: 134 us -> 119 us  [body(): pl.pallas_call(functools.partial(kernel, nz, side), out_shape=jax.ShapeDt...]
where the time goes in v3:
time: 123 us; the launch traced here: 122 us
  Pallas kernels  119 us (97%)
  local copies, waits for them, and re-layouts  2.46 us (2%)
    pallas_call x1, Pallas kernels, body(): pl.pallas_call(functools.partial(kernel, nz, side), out_shape=jax.ShapeDt...  119 us

profile of v3, /device:TPU:1, one launch (start us, length us, event | category | flops | bytes accessed | tf_op | source)
XLA Modules:
  0.0 122.5 jit_solution(17083101259466941648)
XLA Ops:
  0.6 119.4 %shard_map.122 = f32[8,128]{1,0:T(8,128)} custom-call(s32[2,16]{1,0:T(2,128)} %bitcast.2, s32[16]{0:T(128)} %count_hbm.1, s32[16]{0:T(128)} %last_hbm.1, bf16[2,4,64,64]{3,2,1,0:T(8,128)(2,1)} %pages_hbm.1, f32[2,64]{1,0:T(2,128)} %mix_hbm.1, s32[1,128]{1,0:T(1,128)} %target_hbm.1, f32[2,2048]{1,0:T(2,128)} %gain_hbm.1, f32[2,2048]{1,0:T(2,128)} %bias_hbm.1, ...), custom_call_target="tpu_custom_call" | custom-call | tf_op jit(solution)/shard_map/pallas_call | solution.py:787
  120.0 1.3 %constant_dynamic-slice_fusion = f32[1,4]{1,0:T(1,128)} fusion(f32[8,128]{1,0:T(8,128)} %shard_map.122, s32[]{:T(128)S(6)} %select_n.3), kind=kLoop, calls=%fused_computation | loop fusion | bytes 36 | tf_op jit(solution)/shard_map/dynamic_slice | solution.py:843
  121.3 1.2 slice.3

commit v4 on v3

--- a/solution.py
+++ b/solution.py
@@ -11,18 +11,18 @@
 F32 = jnp.float32
 BF16 = jnp.bfloat16
 LANES = 128
-BATCHES = {16: ((0, 8, 4, 12), (1, 15, 7, 9), (2, 14, 6, 10), (3, 13, 5, 11)), 4: ((0, 2), (1, 3))}
+BATCHES = {16: ((0, 1, 15, 2), (14, 3, 13, 8), (4, 12, 7, 9), (5, 11, 6, 10)), 4: ((0, 2), (1, 3))}
 VMEM_LIMIT = 63 * 1024 * 1024
 
 
 ORDER = {4: (0, 1, 3, 2), 2: (0, 1)}
 PARTS = {4: ((0, 3, (1, 3)), (3, 1, (2,))), 2: ((0, 1, ()), (1, 1, (1,)))}
 SCHEDULE = {
-    1: (("s", 0), ("s", 1)),
-    2: (("s", 2),),
-    4: (("s", 3),),
-    5: (("f", 0),),
-    6: (("f", 1), ("r", 0)),
+    0: (("s", 0),),
+    1: (("s", 1), ("s", 2)),
+    2: (("s", 3),),
+    4: (("f", 0),),
+    5: (("f", 1), ("r", 0)),
     7: (("f", 2), ("r", 1)),
     9: (("f", 3), ("r", 2)),
     10: (("r", 3),),
@@ -676,49 +676,6 @@
                 local_stats.at[step], column_stats.at[z], c0_send.at[step], c0_recv, to_z, chip, core
             ).start()
 
-    def combine(parts):
-        peaks = parts[:, 0:1, :]
-        top = jnp.max(peaks, axis=0)
-        sums = jnp.sum(parts[:, 1:2, :] * jnp.exp(peaks - top[None]), axis=0)
-        return top, sums, jnp.sum(parts[:, 2:3, :], axis=0)
-
-    mine = plane_stats.at[core, b]
-
-    @pl.when(a == z_set)
-    def _():
-        await_bytes(column_stats.at[pl.ds(0, nz - 1)], c0_recv)
-        plane_stats[core, b] = rows_of(*combine(column_stats[...]))
-
-        def plane_start(step, carry):
-            to_chip = wrap(chip + step, chips)
-            remote(mine, mine, c1_send.at[0], c1_recv.at[core, b], z, to_chip, core).start()
-            remote(mine, mine, c1_send.at[1], c1_recv.at[core, b], z, to_chip, other).start()
-            return carry
-
-        remote(mine, mine, c1_send.at[1], c1_recv.at[core, b], z, chip, other).start()
-        lax.fori_loop(1, chips, plane_start, 0)
-
-    for of_core in range(2):
-        for at_b in range(side):
-            theirs = plane_stats.at[of_core, at_b]
-            ours = jnp.logical_and(
-                jnp.logical_and(core == of_core, b == at_b), a == z_set
-            )
-
-            @pl.when(jnp.logical_not(ours))
-            def _():
-                await_bytes(theirs, c1_recv.at[of_core, at_b])
-
-    logp = []
-    for of_core in range(2):
-        top, sums_all, hits = combine(plane_stats[of_core])
-        logp.append(hits - top - jnp.log(sums_all))
-    length = (count_ref[z] - 1) * 64 + last_ref[z]
-    valid = iota((1, LANES), 1) < length
-    row = jnp.where(valid, logp[0], 0.0)
-    ratio = jnp.sum(jnp.where(valid, logp[0] - logp[1], 0.0), axis=1, keepdims=True)
-    out_ref[...] = rows_of(row, jnp.broadcast_to(ratio, (1, LANES)))
-
     for copy in pair:
         copy.wait_send()
     for copy in moves + picks + line + cross + sums + crosses + list(sends.values()):
@@ -742,6 +699,49 @@
     if side == 4:
         await_bytes(head_all.at[:, pair_lane(0)], hr_send)
         await_bytes(token_block(0, 0, side), tr_send)
+    def combine(parts):
+        peaks = parts[:, 0:1, :]
+        top = jnp.max(peaks, axis=0)
+        sums = jnp.sum(parts[:, 1:2, :] * jnp.exp(peaks - top[None]), axis=0)
+        return top, sums, jnp.sum(parts[:, 2:3, :], axis=0)
+
+    mine = plane_stats.at[core, b]
+
+    @pl.when(a == z_set)
+    def _():
+        await_bytes(column_stats.at[pl.ds(0, nz - 1)], c0_recv)
+        plane_stats[core, b] = rows_of(*combine(column_stats[...]))
+
+        def plane_start(step, carry):
+            to_chip = wrap(chip + step, chips)
+            remote(mine, mine, c1_send.at[0], c1_recv.at[core, b], z, to_chip, core).start()
+            remote(mine, mine, c1_send.at[1], c1_recv.at[core, b], z, to_chip, other).start()
+            return carry
+
+        remote(mine, mine, c1_send.at[1], c1_recv.at[core, b], z, chip, other).start()
+        lax.fori_loop(1, chips, plane_start, 0)
+
+    for of_core in range(2):
+        for at_b in range(side):
+            theirs = plane_stats.at[of_core, at_b]
+            ours = jnp.logical_and(
+                jnp.logical_and(core == of_core, b == at_b), a == z_set
+            )
+
+            @pl.when(jnp.logical_not(ours))
+            def _():
+                await_bytes(theirs, c1_recv.at[of_core, at_b])
+
+    logp = []
+    for of_core in range(2):
+        top, sums_all, hits = combine(plane_stats[of_core])
+        logp.append(hits - top - jnp.log(sums_all))
+    length = (count_ref[z] - 1) * 64 + last_ref[z]
+    valid = iota((1, LANES), 1) < length
+    row = jnp.where(valid, logp[0], 0.0)
+    ratio = jnp.sum(jnp.where(valid, logp[0] - logp[1], 0.0), axis=1, keepdims=True)
+    out_ref[...] = rows_of(row, jnp.broadcast_to(ratio, (1, LANES)))
+
     for step in range(per_set):
 
         @pl.when(rollouts[step] != z)

time: 123 us -> 121 us (0.984)
    pallas_call x1, Pallas kernels: 119 us -> 118 us  [body(): pl.pallas_call(functools.partial(kernel, nz, side), out_shape=jax.ShapeDt...]
where the time goes in v4:
time: 121 us
  Pallas kernels  118 us (98%)
  local copies, waits for them, and re-layouts  2.46 us (2%)
    pallas_call x1, Pallas kernels, body(): pl.pallas_call(functools.partial(kernel, nz, side), out_shape=jax.ShapeDt...  118 us

profile of v4, /device:TPU:1, one launch (start us, length us, event | category | flops | bytes accessed | tf_op | source)
XLA Modules:
  0.0 121.2 jit_solution(8748073063258733128)
XLA Ops:
  0.6 118.1 %shard_map.122 = f32[8,128]{1,0:T(8,128)} custom-call(s32[2,16]{1,0:T(2,128)} %bitcast.2, s32[16]{0:T(128)} %count_hbm.1, s32[16]{0:T(128)} %last_hbm.1, bf16[2,4,64,64]{3,2,1,0:T(8,128)(2,1)} %pages_hbm.1, f32[2,64]{1,0:T(2,128)} %mix_hbm.1, s32[1,128]{1,0:T(1,128)} %target_hbm.1, f32[2,2048]{1,0:T(2,128)} %gain_hbm.1, f32[2,2048]{1,0:T(2,128)} %bias_hbm.1, ...), custom_call_target="tpu_custom_call" | custom-call | tf_op jit(solution)/shard_map/pallas_call | solution.py:787
  118.8 1.3 %constant_dynamic-slice_fusion = f32[1,4]{1,0:T(1,128)} fusion(f32[8,128]{1,0:T(8,128)} %shard_map.122, s32[]{:T(128)S(6)} %select_n.3), kind=kLoop, calls=%fused_computation | loop fusion | bytes 36 | tf_op jit(solution)/shard_map/dynamic_slice | solution.py:843
  120.0 1.2 slice.3

commit v5 on v4

--- a/solution.py
+++ b/solution.py
@@ -560,12 +560,12 @@
     def token_cols(at_b, at_a):
         return lane(at_b * side + at_a)
 
-    def token_copy(first, size, at_a, to_z):
+    def token_copy(index, first, size, at_a, to_z):
         return remote(
             sets.at[pl.ds(first, size)],
             tokens.at[pl.ds(first, size), :, token_cols(b, at_a)],
             ta_send,
-            ta_recv.at[at_a],
+            ta_recv.at[index, at_a],
             to_z,
             chip_at(z_set, b),
             core,
@@ -576,7 +576,7 @@
             sends[step].wait_recv()
         for offset in reversed((0,) + near):
             if offset:
-                token_copy(first, size, a, wrap(z - sign * offset, nz)).start()
+                token_copy(index, first, size, a, wrap(z - sign * offset, nz)).start()
                 continue
 
             @pl.when(gap == 0)
@@ -585,7 +585,7 @@
 
             @pl.when(gap != 0)
             def _():
-                token_copy(first, size, a, z).start()
+                token_copy(index, first, size, a, z).start()
 
         at(8 + index)
 
@@ -597,34 +597,46 @@
 
     half = side // 2
 
-    def token_block(at_b, first, size):
+    def token_block(index, at_b, first, size):
         start = pl.multiple_of((at_b * side + first) * LANES, LANES)
-        return tokens.at[:, :, pl.ds(start, size * LANES)]
-
-    for at_a in range(side):
-
-        @pl.when(jnp.logical_not(jnp.logical_and(gap == 0, a == at_a)))
-        def _():
-            await_bytes(tokens.at[:, :, pl.ds(0, LANES)], ta_recv.at[at_a])
-
-    for turn in range(2):
+        low, height, _ = parts[index]
+        return tokens.at[pl.ds(low, height), :, pl.ds(start, size * LANES)]
+
+    for index, (first, size, _) in enumerate(parts):
+        for at_a in range(side):
+
+            @pl.when(jnp.logical_not(jnp.logical_and(gap == 0, a == at_a)))
+            def _():
+                await_bytes(token_block(index, 0, 0, 1), ta_recv.at[index, at_a])
+
+        for turn in range(2):
+            for place, slot in ring:
+                block = token_block(index, b, (turn + slot) % 2 * half, half)
+                remote(
+                    block,
+                    block,
+                    tb_send.at[slot, index],
+                    tb_recv.at[slot, index, turn],
+                    z,
+                    across(place),
+                    core,
+                ).start()
+    at(10)
+    for index in range(len(parts)):
         for place, slot in ring:
-            part = (turn + slot) % 2
-            block = token_block(b, part * half, half)
-            remote(
-                block, block, tb_send.at[slot], tb_recv.at[slot, turn], z, across(place), core
-            ).start()
-    at(10)
-    if side == 4:
-        for place, slot in ring:
-            await_bytes(token_block(0, 0, half), tb_recv.at[slot, 0])
-            block = token_block(wrap(b - place, side), slot * half, half)
-            remote(block, block, tr_send, tr_recv.at[slot], z, across(place), core).start()
-    else:
-        await_bytes(token_block(0, 0, half), tb_recv.at[0, 0])
+            await_bytes(token_block(index, 0, 0, half), tb_recv.at[slot, index, 0])
+            if side == 4:
+                block = token_block(index, wrap(b - place, side), slot * half, half)
+                remote(
+                    block,
+                    block,
+                    tr_send.at[index],
+                    tr_recv.at[slot, index],
+                    z,
+                    across(place),
+                    core,
+                ).start()
     at(11)
-    for place, slot in ring:
-        await_bytes(token_block(0, 0, half), tb_recv.at[slot, 1])
     if side == 4:
         for place, slot in ring:
             for batch, steps_in in enumerate(batches):
@@ -632,19 +644,37 @@
                     head_all.at[0 : len(steps_in) // 2 * rows, pair_lane(0)],
                     hr_recv.at[slot, batch],
                 )
+
+    depth = side * LANES
+
+    def add_logits(place, first):
+        cols = pl.ds(pl.multiple_of(wrap(b + place, side) * depth, depth), depth)
+
+        def block_step(block, carry):
+            part = jnp.dot(
+                tokens[:, :, cols].reshape(count, depth),
+                head_all[cols, pair_lane(block)],
+                preferred_element_type=F32,
+            )
+            logits[block] = part if first else logits[block] + part
+            return carry
+
+        lax.fori_loop(0, side, block_step, 0)
+
+    add_logits(0, True)
+    for place, slot in ring:
+        for index in range(len(parts)):
+            await_bytes(token_block(index, 0, 0, half), tb_recv.at[slot, index, 1])
+        add_logits(-place, False)
+    if side == 4:
         for place, slot in ring:
-            await_bytes(token_block(0, 0, half), tr_recv.at[slot])
-
-    def make_logits(block, peak):
-        part = jnp.dot(
-            tokens[...].reshape(count, width),
-            head_all[:, pair_lane(block)],
-            preferred_element_type=F32,
-        )
-        logits[block] = part
-        return jnp.maximum(peak, jnp.maximum(part[:, :LANES], part[:, LANES:]))
-
-    peak = lax.fori_loop(0, side, make_logits, jnp.full((count, LANES), -jnp.inf, F32))
+            for index in range(len(parts)):
+                await_bytes(token_block(index, 0, 0, half), tr_recv.at[slot, index])
+        add_logits(2, False)
+    peak = jnp.full((count, LANES), -jnp.inf, F32)
+    for block in range(side):
+        part = logits[block]
+        peak = jnp.maximum(peak, jnp.maximum(part[:, :LANES], part[:, LANES:]))
     peak = jnp.max(peak, axis=1, keepdims=True)
     total = jnp.zeros((count, LANES), F32)
     hit = jnp.zeros((count, LANES), F32)
@@ -685,7 +715,8 @@
     await_bytes(head_all.at[0 : (nz - 1) * rows, pair_lane(0)], hz_send)
     for place, slot in ring:
         await_bytes(head_all.at[:, pair_lane(0)], hf_send.at[slot])
-        await_bytes(token_block(0, 0, side), tb_send.at[slot])
+        for index in range(len(parts)):
+            await_bytes(token_block(index, 0, 0, side), tb_send.at[slot, index])
     sent = tokens.at[:, :, pl.ds(0, len(near) * LANES)]
 
     @pl.when(gap == 0)
@@ -698,7 +729,8 @@
 
     if side == 4:
         await_bytes(head_all.at[:, pair_lane(0)], hr_send)
-        await_bytes(token_block(0, 0, side), tr_send)
+        for index in range(len(parts)):
+            await_bytes(token_block(index, 0, 0, side), tr_send.at[index])
     def combine(parts):
         peaks = parts[:, 0:1, :]
         top = jnp.max(peaks, axis=0)
@@ -782,7 +814,7 @@
     semaphores = [6, 6, 14, (), ()]
     semaphores += [4] * 2 + [per_set] * 2 + [side] * 8
     semaphores += [(), (), (), batches, 2, (2, batches), (), (2, batches)]
-    semaphores += [per_set] * 2 + [(), side, 2, (2, 2), (), 2]
+    semaphores += [per_set] * 2 + [(), (2, side), (2, 2), (2, 2, 2), 2, (2, 2)]
     semaphores += [per_set, (), 2, (2, side)]
     result = pl.pallas_call(
         functools.partial(kernel, nz, side),

time: 121 us -> 122 us (level)
  no operation moved by 1% of the time
where the time goes in v5:
time: 122 us; the launch traced here: 121 us
  Pallas kernels  118 us (97%)
  local copies, waits for them, and re-layouts  2.46 us (2%)
    pallas_call x1, Pallas kernels, body(): pl.pallas_call(functools.partial(kernel, nz, side), out_shape=jax.ShapeDt...  118 us

profile of v5, /device:TPU:1, one launch (start us, length us, event | category | flops | bytes accessed | tf_op | source)
XLA Modules:
  0.0 121.4 jit_solution(8020979252014196007)
XLA Ops:
  0.6 118.2 %shard_map.122 = f32[8,128]{1,0:T(8,128)} custom-call(s32[2,16]{1,0:T(2,128)} %bitcast.2, s32[16]{0:T(128)} %count_hbm.1, s32[16]{0:T(128)} %last_hbm.1, bf16[2,4,64,64]{3,2,1,0:T(8,128)(2,1)} %pages_hbm.1, f32[2,64]{1,0:T(2,128)} %mix_hbm.1, s32[1,128]{1,0:T(1,128)} %target_hbm.1, f32[2,2048]{1,0:T(2,128)} %gain_hbm.1, f32[2,2048]{1,0:T(2,128)} %bias_hbm.1, ...), custom_call_target="tpu_custom_call" | custom-call | tf_op jit(solution)/shard_map/pallas_call | solution.py:819
  118.9 1.3 %constant_dynamic-slice_fusion = f32[1,4]{1,0:T(1,128)} fusion(f32[8,128]{1,0:T(8,128)} %shard_map.122, s32[]{:T(128)S(6)} %select_n.3), kind=kLoop, calls=%fused_computation | loop fusion | bytes 36 | tf_op jit(solution)/shard_map/dynamic_slice | solution.py:875
  120.2 1.2 slice.3
